TPU v7x, 32 devices: a whole 2x2x4 slice. The times are simulated.
32 devices in a mesh: sp: 8 (over z, y), ch: 4 (over x, core).
Axes of the slice: x: 2, y: 2, z: 4, core: 2. Of those that a mesh axis runs over, the one named last changes fastest.
Arguments:
- inputs: bfloat16 [2, 256, 1024, 1024], P(None, 'ch', 'sp'), may hold values from -6 to 6
- cotangent: bfloat16 [2, 256, 1024, 1024], P(None, 'ch', 'sp'), may hold values from -6 to 6
- input_factor: bfloat16 [256, 26], P('ch'), may hold values from -0.375 to 0.375
- output_factor: bfloat16 [256, 26], P('ch'), may hold values from -0.375 to 0.375
- height_factor: float32 [96, 10], replicated, may hold values from -0.625 to 0.625
- width_factor: float32 [96, 10], replicated, may hold values from -0.625 to 0.625
- core_tensor: float32 [2, 26, 26, 10, 10], replicated, may hold values from -0.078125 to 0.078125
Outputs:
- core_grad: float32 [2, 26, 26, 10, 10], replicated
- input_grad: float32 [256, 26], P('ch')
- output_grad: float32 [256, 26], P('ch')
- height_grad: float32 [96, 10], replicated
- width_grad: float32 [96, 10], replicated
All inputs are finite; a program needn't handle non-finite values.
Results may differ from a plain program's by a relative error of at most 0.0086.
Values may be sent and summed in bfloat16 or wider, within the bound.
No kernel may reach another device: no remote copies, remote signals or barrier semaphores. Data moves between devices by JAX's collectives and lax.ppermute only.
A program may use at most 448 MiB of HBM per device.

v0:
```python
import math

import jax
import jax.numpy as jnp
from jax import lax
from jax.sharding import PartitionSpec as P

precise = lax.Precision.HIGHEST


def product(form, *operands):
    return jnp.einsum(form, *operands, precision=precise)


def row_table(width, modes):
    columns = jnp.arange(width, dtype=jnp.int32)[:, None]
    frequency = jnp.arange(modes, dtype=jnp.int32)[None, :]
    phases = (columns * frequency % width).astype(jnp.float32)
    angles = phases * (2.0 * math.pi / width)
    scaling = 1.0 / math.sqrt(width)
    cosine = jnp.cos(angles) * scaling
    minus_sine = -jnp.sin(angles) * scaling
    return jnp.stack([cosine, minus_sine], axis=1).astype(jnp.bfloat16)


def column_table(height, kept):
    halfway = kept // 2
    ordinal = jnp.arange(kept, dtype=jnp.int32)
    frequency = jnp.where(ordinal < halfway, ordinal, ordinal + (height - kept))
    heights = jnp.arange(height, dtype=jnp.int32)
    phases = (frequency[:, None] * heights[None, :] % height).astype(jnp.float32)
    angles = phases * (2.0 * math.pi / height)
    scaling = 1.0 / math.sqrt(height)
    cosine = jnp.cos(angles) * scaling
    sines = jnp.sin(angles) * scaling
    upper = jnp.concatenate([cosine, sines], axis=1)
    lower = jnp.concatenate([-sines, cosine], axis=1)
    return jnp.concatenate([upper, lower], axis=0).astype(jnp.bfloat16)


def contract(spectra, factor):
    return jnp.einsum("bipm,ia->bapm", spectra, factor, preferred_element_type=jnp.float32)


def selectors(start, count, kept, modes):
    ordinal = start + jnp.arange(count, dtype=jnp.int32)
    height_pick = (
        (ordinal // modes)[:, None] == jnp.arange(kept, dtype=jnp.int32)[None, :]
    ).astype(jnp.float32)
    width_pick = ((ordinal % modes)[:, None] == jnp.arange(modes, dtype=jnp.int32)[None, :]).astype(
        jnp.float32
    )
    return (height_pick, width_pick)


def owner_work(left, right, core_tensor, height_factor, width_factor, height_pick, width_pick):
    height_rows = jnp.dot(height_pick, height_factor, precision=precise)
    width_rows = jnp.dot(width_pick, width_factor, precision=precise)
    left_real = left[:, :, 0]
    left_imag = -left[:, :, 1]
    right_real = right[:, :, 0]
    right_imag = right[:, :, 1]
    pair_real = product("bam,bem->aem", left_real, right_real) - product(
        "bam,bem->aem", left_imag, right_imag
    )
    pair_imag = product("bam,bem->aem", left_real, right_imag) + product(
        "bam,bem->aem", left_imag, right_real
    )
    folded_real = product("aecd,md->aecm", core_tensor[0], width_rows)
    folded_imag = product("aecd,md->aecm", core_tensor[1], width_rows)
    turned_real = product("aecd,mc->aedm", core_tensor[0], height_rows)
    turned_imag = product("aecd,mc->aedm", core_tensor[1], height_rows)
    modal_real = product("aecm,mc->aem", folded_real, height_rows)
    modal_imag = product("aecm,mc->aem", folded_imag, height_rows)
    core_part = jnp.stack(
        [
            product("aem,mc,md->aecd", pair_real, height_rows, width_rows),
            product("aem,mc,md->aecd", pair_imag, height_rows, width_rows),
        ],
        axis=0,
    )
    height_terms = product("aem,aecm->mc", pair_real, folded_real) + product(
        "aem,aecm->mc", pair_imag, folded_imag
    )
    height_part = product("mk,mc->kc", height_pick, height_terms)
    width_terms = product("aem,aedm->md", pair_real, turned_real) + product(
        "aem,aedm->md", pair_imag, turned_imag
    )
    width_part = product("ml,md->ld", width_pick, width_terms)
    inward_real = product("aem,bem->bam", modal_real, right_real) + product(
        "aem,bem->bam", modal_imag, right_imag
    )
    inward_imag = product("aem,bem->bam", modal_real, right_imag) - product(
        "aem,bem->bam", modal_imag, right_real
    )
    outward_real = product("aem,bam->bem", modal_real, left_real) + product(
        "aem,bam->bem", modal_imag, left_imag
    )
    outward_imag = product("aem,bam->bem", modal_real, left_imag) - product(
        "aem,bam->bem", modal_imag, left_real
    )
    inward = jnp.stack([inward_real, inward_imag], axis=2).astype(jnp.bfloat16)
    outward = jnp.stack([outward_real, outward_imag], axis=2).astype(jnp.bfloat16)
    return (core_part, height_part, width_part, inward, outward)


def block_grads(owner_input, owner_cot, inward, outward):
    input_part = jnp.einsum(
        "bipm,bapm->ia", owner_input, inward, preferred_element_type=jnp.float32
    )
    signed = jnp.stack([owner_cot[:, :, 0], -owner_cot[:, :, 1]], axis=2)
    output_part = jnp.einsum("bopm,bepm->oe", signed, outward, preferred_element_type=jnp.float32)
    return (input_part, output_part)


def on_device(
    inputs, cotangent, input_factor, output_factor, height_factor, width_factor, core_tensor
):
    batch, channels, rows_here, width = inputs.shape
    kept = height_factor.shape[0]
    modes = width_factor.shape[0]
    shards = lax.axis_size("sp")
    height = rows_here * shards
    items = batch * channels
    owned = kept * modes // shards
    row_weights = row_table(width, modes)
    column_weights = column_table(height, kept)

    def to_rows(field):
        return jnp.einsum(
            "nhw,wpl->nphl", field, row_weights, preferred_element_type=jnp.float32
        ).astype(jnp.bfloat16)

    def to_columns(piece):
        stacked = piece.reshape(piece.shape[0], 2 * piece.shape[2], piece.shape[3])
        return jnp.einsum(
            "kh,nhl->nkl", column_weights, stacked, preferred_element_type=jnp.float32
        ).astype(jnp.bfloat16)

    flat_input = inputs.reshape(items, rows_here, width)
    flat_cot = cotangent.reshape(items, rows_here, width)
    spec_input = to_columns(
        lax.all_to_all(to_rows(flat_input), "sp", split_axis=0, concat_axis=2, tiled=True)
    )
    spec_cot = to_columns(
        lax.all_to_all(to_rows(flat_cot), "sp", split_axis=0, concat_axis=2, tiled=True)
    )
    local_count = spec_input.shape[0]
    spec_input = spec_input.reshape(local_count, 2, kept * modes)
    spec_cot = spec_cot.reshape(local_count, 2, kept * modes)
    owner_input, owner_cot = (
        lax.all_to_all(spec_input, "sp", split_axis=2, concat_axis=0, tiled=True),
        lax.all_to_all(spec_cot, "sp", split_axis=2, concat_axis=0, tiled=True),
    )
    owner_input = owner_input.reshape(batch, channels, 2, owned)
    owner_cot = owner_cot.reshape(batch, channels, 2, owned)
    left = contract(owner_input, input_factor)
    right = contract(owner_cot, output_factor)
    start = lax.axis_index("sp") * owned
    left, right = lax.psum((left, right), "ch")
    height_pick, width_pick = selectors(start, owned, kept, modes)
    core_part, height_part, width_part, inward, outward = owner_work(
        left, right, core_tensor, height_factor, width_factor, height_pick, width_pick
    )
    input_part, output_part = block_grads(owner_input, owner_cot, inward, outward)
    core_grad, height_grad, width_grad, input_grad, output_grad = lax.psum(
        (core_part, height_part, width_part, input_part, output_part), "sp"
    )
    return (core_grad, input_grad, output_grad, height_grad, width_grad)


def solution(mesh):
    placed = (
        P(None, "ch", "sp", None),
        P(None, "ch", "sp", None),
        P("ch", None),
        P("ch", None),
        P(),
        P(),
        P(),
    )
    return jax.shard_map(
        on_device,
        mesh=mesh,
        in_specs=placed,
        out_specs=(P(), P("ch", None), P("ch", None), P(), P()),
        check_vma=False,
    )
```

profile of v0, /device:TPU:0, one launch (start us, length us, event | category | flops | bytes accessed | tf_op | source)
XLA Modules:
  0.0 1142.8 jit_solution(15091796225793856751)
XLA Ops:
  8.8 18.2 %convert_bitcast_fusion = bf16[128,2,128,96]{2,3,0,1:T(8,128)(2,1)} fusion(bf16[128,128,1024,1]{2,1,0,3:T(8,128)(2,1)} %bitcast.261, bf16[1024,1,96]{0,2,1:T(8,128)(2,1)S(1)} %get-tuple-element.57, bf16[1024,1,96]{0,2,1:T(8,128)(2,1)S(1)} %get-tuple-element.58), kind=kOutput, calls=%fused_computation.28 | convolution fusion | flops 6446383104 | bytes 40239104 | tf_op jit(solution)/shard_map/nhw,wpl->nphl/dot_general | solution.py:130
  42.0 18.3 %convert_bitcast_fusion.1 = bf16[128,2,128,96]{2,3,0,1:T(8,128)(2,1)} fusion(bf16[128,128,1024,1]{2,1,0,3:T(8,128)(2,1)} %bitcast.262, bf16[1024,1,96]{0,2,1:T(8,128)(2,1)S(1)} %get-tuple-element.57, bf16[1024,1,96]{0,2,1:T(8,128)(2,1)S(1)} %get-tuple-element.58), kind=kOutput, calls=%fused_computation.29 | convolution fusion | flops 6446383104 | bytes 40239104 | tf_op jit(solution)/shard_map/nhw,wpl->nphl/dot_general | solution.py:130
  67.9 112.3 %all-to-all-done.2 = bf16[128,2,128,96]{2,3,1,0:T(8,128)(2,1)} async-done(((bf16[128,2,128,96]{2,3,1,0:T(8,128)(2,1)}), bf16[128,2,128,96]{2,3,1,0:T(8,128)(2,1)}, u32[]{:S(2)}, u32[]{:S(2)}) %all-to-all-start.2) | async-done | bytes 6291488 | tf_op jit(solution)/shard_map/all_to_all | solution.py:143
  228.9 93.6 %all-to-all-done = bf16[128,2,128,96]{2,3,1,0:T(8,128)(2,1)} async-done(((bf16[128,2,128,96]{2,3,1,0:T(8,128)(2,1)}), bf16[128,2,128,96]{2,3,1,0:T(8,128)(2,1)}, u32[]{:S(2)}, u32[]{:S(2)}) %all-to-all-start) | async-done | bytes 6291488 | tf_op jit(solution)/shard_map/all_to_all | solution.py:146
  322.5 14.8 %all-to-all-start.3 = ((bf16[8,2,18432]{2,1,0:T(2,128)(2,1)}), bf16[8,2,18432]{2,1,0:T(2,128)(2,1)S(1)}, u32[]{:S(2)}, u32[]{:S(2)}) async-start(bf16[8,2,18432]{2,1,0:T(2,128)(2,1)} %reshape.175), calls=%async_computation.3 | async-start | bytes 1179648 | tf_op jit(solution)/shard_map/all_to_all | solution.py:152
  424.5 37.8 %all-reduce.7.cloned.1.call-done = (f32[2,26,2,1152]{3,1,2,0:T(8,128)}, f32[2,26,2,1152]{3,1,2,0:T(8,128)}) async-done(((f32[2,26,2,1152]{3,1,2,0:T(8,128)}, f32[2,26,2,1152]{3,1,2,0:T(8,128)}), (f32[2,26,2,1152]{3,1,2,0:T(8,128)}, f32[2,26,2,1152]{3,1,2,0:T(8,128)})) %all-reduce.7.cloned.1.call-update) | async-done | bytes 958480 | tf_op jit(solution)/shard_map/psum | solution.py:160
  471.0 31.0 %fusion.123 = f32[1152,26,26]{2,1,0:T(8,128)S(1)} fusion(f32[2,26,1152]{1,0,2:T(2,128)S(1)} %copy.221, f32[2,26,1152]{1,0,2:T(2,128)} %copy.220), kind=kOutput, calls=%fused_computation.149 | convolution fusion | flops 18690048 | bytes 3594240 | tf_op jit(solution)/shard_map/bam,bem->aem/dot_general | solution.py:12
  502.0 32.7 %fusion.122 = f32[1152,26,26]{2,1,0:T(8,128)} fusion(f32[2,26,1152]{1,0,2:T(2,128)S(1)} %copy.219, f32[2,26,1152]{1,0,2:T(2,128)S(1)} %copy-done.4), kind=kOutput, calls=%fused_computation.148 | convolution fusion | flops 18690048 | bytes 3594240 | tf_op jit(solution)/shard_map/bam,bem->aem/dot_general | solution.py:12
  534.7 32.8 %convolution_add_fusion = f32[1152,26,26]{2,1,0:T(8,128)} fusion(f32[1152,26,26]{2,1,0:T(8,128)S(1)} %fusion.123, f32[2,26,1152]{1,0,2:T(2,128)S(1)} %copy.219, f32[2,26,1152]{1,0,2:T(2,128)S(1)} %copy.222), kind=kOutput, calls=%fused_computation.24 | convolution fusion | flops 19468800 | bytes 6709248 | tf_op jit(solution)/shard_map/bam,bem->aem/dot_general | solution.py:12
  567.5 15.6 %copy.308 = f32[1152,26,26]{0,2,1:T(8,128)} copy(f32[1152,26,26]{1,2,0:T(8,128)} %bitcast.247) | data formatting | bytes 6230016
  583.0 34.6 %multiply_reduce_fusion = f32[1152,10]{0,1:T(8,128)} fusion(f32[1152,26,26]{0,2,1:T(8,128)} %copy.308, f32[1,26,26,10,10]{2,0,4,3,1:T(1,128)} %get-tuple-element.43, f32[1152,10]{0,1:T(8,128)} %fusion.77), kind=kOutput, calls=%fused_computation.4 | convolution fusion | flops 950065920 | bytes 3477568 | tf_op jit(solution)/shard_map/aecd,mc->aedm/dot_general | solution.py:12
  617.6 36.4 %multiply_reduce_fusion.2 = (f32[1152,10]{0,1:T(8,128)}, f32[1152,26,26,10]{0,2,3,1:T(8,128)}) fusion(f32[1152,26,26]{0,2,1:T(8,128)S(1)} %copy-done.8, f32[1,26,26,10,10]{2,0,4,3,1:T(1,128)S(1)} %copy-done.12, f32[1152,10]{0,1:T(8,128)S(1)} %copy-done.18), kind=kOutput, calls=%fused_computation.6 | convolution fusion | flops 950065920 | bytes 34627648 | tf_op jit(solution)/shard_map/aecd,md->aecm/dot_general | solution.py:12
  654.1 46.2 %fusion.1 = (f32[1152,26,26]{0,2,1:T(8,128)}, f32[1152,26,26]{0,2,1:T(8,128)}, f32[1152,26,26,10]{0,2,3,1:T(8,128)}) fusion(f32[1152,10]{0,1:T(8,128)S(1)} %copy-done.17, f32[1152,26,26,10]{0,2,3,1:T(8,128)} %get-tuple-element.56, f32[1,26,26,10,10]{2,0,4,3,1:T(1,128)S(1)} %copy-done.7, f32[1152,10]{0,1:T(8,128)S(1)} %copy-done.18), kind=kOutput, calls=%fused_computation.3 | convolution fusion | flops 964094976 | bytes 68892736 | tf_op jit(solution)/shard_map/aecd,md->aecm/dot_general | solution.py:12
  700.3 16.2 %copy.263 = f32[1152,26,26]{2,1,0:T(8,128)} copy(f32[1152,26,26]{0,2,1:T(8,128)} %get-tuple-element.36) | data formatting | bytes 6230016 | tf_op jit(solution)/shard_map/aecm,mc->aem/dot_general | solution.py:12
  716.5 33.8 %fusion.6 = f32[1152,2,26]{2,1,0:T(2,128)} fusion(f32[2,26,1152]{1,0,2:T(2,128)S(1)} %copy.219, f32[1152,26,26]{2,1,0:T(8,128)} %copy.263), kind=kOutput, calls=%fused_computation.12 | convolution fusion | flops 18690048 | bytes 3594240 | tf_op jit(solution)/shard_map/aem,bem->bam/dot_general | solution.py:12
  750.3 30.9 %fusion.8 = f32[1152,2,26]{2,1,0:T(2,128)} fusion(f32[2,26,1152]{1,0,2:T(2,128)S(1)} %copy.221, f32[1152,26,26]{2,1,0:T(8,128)S(1)} %copy-done.2), kind=kOutput, calls=%fused_computation.14 | convolution fusion | flops 18690048 | bytes 3594240 | tf_op jit(solution)/shard_map/aem,bem->bam/dot_general | solution.py:12
  781.2 16.0 %fusion.4 = f32[1152,2,26]{2,1,0:T(2,128)} fusion(f32[2,26,1152]{1,0,2:T(2,128)S(1)} %copy.222, f32[1152,26,26]{2,1,0:T(8,128)S(1)} %copy-done.2), kind=kOutput, calls=%fused_computation.10 | convolution fusion | flops 18690048 | bytes 3594240 | tf_op jit(solution)/shard_map/aem,bam->bem/dot_general | solution.py:12
  797.2 16.2 %fusion.2 = f32[1152,2,26]{2,1,0:T(2,128)} fusion(f32[2,26,1152]{1,0,2:T(2,128)S(1)} %copy-done.5, f32[1152,26,26]{2,1,0:T(8,128)S(1)} %copy-done.2), kind=kOutput, calls=%fused_computation.8 | convolution fusion | flops 18690048 | bytes 3594240 | tf_op jit(solution)/shard_map/aem,bam->bem/dot_general | solution.py:12
  813.4 15.6 %copy.228 = f32[26,26,1152]{2,1,0:T(8,128)} copy(f32[26,26,1152]{0,1,2:T(8,128)} %bitcast.248) | data formatting | bytes 6230016 | tf_op jit(solution)/shard_map/add | solution.py:66
  829.0 12.2 %fusion.31 = f32[1,26,26,10,10]{2,3,1,4,0:T(8,128)} fusion(f32[26,26,1152]{2,1,0:T(8,128)} %copy.228, f32[1152,10]{0,1:T(8,128)} %fusion.77, f32[1152,10]{0,1:T(8,128)} %fusion.78), kind=kOutput, calls=%fused_computation.46 | convolution fusion | flops 934617600 | bytes 3477568 | tf_op jit(solution)/shard_map/aem,mc,md->aecd/dot_general | solution.py:12
  841.2 34.6 %convolution_subtract_fusion = f32[1152,26,26]{2,1,0:T(8,128)} fusion(f32[1152,26,26]{2,1,0:T(8,128)} %fusion.122, f32[2,26,1152]{1,0,2:T(2,128)S(1)} %copy.221, f32[2,26,1152]{1,0,2:T(2,128)S(1)} %copy.222), kind=kOutput, calls=%fused_computation.25 | convolution fusion | flops 19468800 | bytes 6709248 | tf_op jit(solution)/shard_map/bam,bem->aem/dot_general | solution.py:12
  875.8 15.6 %copy.307 = f32[1152,26,26]{0,2,1:T(8,128)} copy(f32[1152,26,26]{1,2,0:T(8,128)} %bitcast.249) | data formatting | bytes 6230016
  891.4 34.1 %multiply_reduce_fusion.1 = f32[1152,10]{0,1:T(8,128)} fusion(f32[1152,26,26]{0,2,1:T(8,128)} %copy.307, f32[1,26,26,10,10]{2,0,4,3,1:T(1,128)} %get-tuple-element.44, f32[1152,10]{0,1:T(8,128)} %fusion.77), kind=kOutput, calls=%fused_computation.5 | convolution fusion | flops 950065920 | bytes 3477568 | tf_op jit(solution)/shard_map/aecd,mc->aedm/dot_general | solution.py:12
  925.5 16.0 %copy.223 = f32[26,26,1152]{2,1,0:T(8,128)} copy(f32[26,26,1152]{0,1,2:T(8,128)} %bitcast.250) | data formatting | bytes 6230016 | tf_op jit(solution)/shard_map/sub | solution.py:63
  941.5 10.8 fusion.28
  954.8 16.8 %multiply_reduce_fusion.3 = f32[1152,10]{0,1:T(8,128)} fusion(f32[1152,26,26,10]{0,2,3,1:T(8,128)} %get-tuple-element.54, f32[1152,26,26]{0,2,1:T(8,128)} %copy.307), kind=kLoop, calls=%fused_computation.7 | loop fusion | flops 15563520 | bytes 34311168
  971.6 16.2 %copy.257 = f32[1152,26,26]{2,1,0:T(8,128)} copy(f32[1152,26,26]{0,2,1:T(8,128)} %get-tuple-element.35) | data formatting | bytes 6230016 | tf_op jit(solution)/shard_map/aecm,mc->aem/dot_general | solution.py:12
  987.8 33.1 %fusion.47 = bf16[2,26,1,1152]{1,0,3,2:T(2,128)(2,1)S(1)} fusion(f32[1152,2,26]{2,1,0:T(2,128)} %fusion.6, f32[2,26,1152]{1,0,2:T(2,128)S(1)} %copy.221, f32[1152,26,26]{2,1,0:T(8,128)} %copy.257), kind=kOutput, calls=%fused_computation.62 | convolution fusion | flops 18809856 | bytes 3714048 | tf_op jit(solution)/shard_map/aem,bem->bam/dot_general | solution.py:12
  1021.0 30.0 %fusion.42 = bf16[2,26,1,1152]{1,0,3,2:T(2,128)(2,1)S(1)} fusion(f32[1152,2,26]{2,1,0:T(2,128)S(1)} %copy-done.11, f32[2,26,1152]{1,0,2:T(2,128)S(1)} %copy.219, f32[1152,26,26]{2,1,0:T(8,128)S(1)} %copy-done.3), kind=kOutput, calls=%fused_computation.61 | convolution fusion | flops 18809856 | bytes 3714048 | tf_op jit(solution)/shard_map/aem,bem->bam/dot_general | solution.py:12
  1053.6 15.2 %fusion.52 = bf16[2,26,1,1152]{1,0,3,2:T(2,128)(2,1)S(1)} fusion(f32[1152,2,26]{2,1,0:T(2,128)S(1)} %copy-done.10, f32[2,26,1152]{1,0,2:T(2,128)S(1)} %copy-done.6, f32[1152,26,26]{2,1,0:T(8,128)S(1)} %copy-done.3), kind=kOutput, calls=%fused_computation.63 | convolution fusion | flops 18809856 | bytes 3714048 | tf_op jit(solution)/shard_map/aem,bam->bem/dot_general | solution.py:12
  1068.8 15.5 %fusion.57 = bf16[2,26,1,1152]{1,0,3,2:T(2,128)(2,1)S(1)} fusion(f32[1152,2,26]{2,1,0:T(2,128)S(1)} %copy-done.9, f32[2,26,1152]{1,0,2:T(2,128)S(1)} %copy.222, f32[1152,26,26]{2,1,0:T(8,128)S(1)} %copy-done.3), kind=kOutput, calls=%fused_computation.64 | convolution fusion | flops 18809856 | bytes 3714048 | tf_op jit(solution)/shard_map/aem,bam->bem/dot_general | solution.py:12
  1089.6 40.1 %all-reduce = (f32[64,26]{0,1:T(8,128)}, f32[64,26]{0,1:T(8,128)}, f32[96,10]{0,1:T(8,128)}, f32[96,10]{0,1:T(8,128)}) all-reduce(f32[64,26]{0,1:T(8,128)S(1)} %fusion.60, f32[64,26]{0,1:T(8,128)S(1)} %fusion.63, f32[96,10]{0,1:T(8,128)S(1)} %fusion.75, f32[96,10]{0,1:T(8,128)S(1)} %fusion.73), channel_id=1, replica_groups=mesh['sp'=8,'ch'=4] {'sp'}, use_global_device_ids=true, to_apply=%region_3.4 | all-reduce | flops 5248 | bytes 41984 | tf_op jit(solution)/shard_map/psum | solution.py:166
  (122 shorter events, 184.5 us)
Async XLA Ops:
  7.2 413.8 %copy-start = (bf16[64,26]{0,1:T(8,128)(2,1)S(1)}, bf16[64,26]{0,1:T(8,128)(2,1)}, u32[]{:S(2)}) copy-start(bf16[64,26]{0,1:T(8,128)(2,1)} %param.9) | copy-start | bytes 9988
  34.7 145.5 %all-to-all-start.2 = ((bf16[128,2,128,96]{2,3,1,0:T(8,128)(2,1)}), bf16[128,2,128,96]{2,3,1,0:T(8,128)(2,1)}, u32[]{:S(2)}, u32[]{:S(2)}) async-start(bf16[128,2,128,96]{2,3,1,0:T(8,128)(2,1)} %copy.212), calls=%async_computation.2 | async-start | bytes 12582912 | tf_op jit(solution)/shard_map/all_to_all | solution.py:143
  180.2 142.3 %all-to-all-start = ((bf16[128,2,128,96]{2,3,1,0:T(8,128)(2,1)}), bf16[128,2,128,96]{2,3,1,0:T(8,128)(2,1)}, u32[]{:S(2)}, u32[]{:S(2)}) async-start(bf16[128,2,128,96]{2,3,1,0:T(8,128)(2,1)} %copy.205), calls=%async_computation | async-start | bytes 12582912 | tf_op jit(solution)/shard_map/all_to_all | solution.py:146
  322.5 56.9 %all-to-all-start.3 = ((bf16[8,2,18432]{2,1,0:T(2,128)(2,1)}), bf16[8,2,18432]{2,1,0:T(2,128)(2,1)S(1)}, u32[]{:S(2)}, u32[]{:S(2)}) async-start(bf16[8,2,18432]{2,1,0:T(2,128)(2,1)} %reshape.175), calls=%async_computation.3 | async-start | bytes 1179648 | tf_op jit(solution)/shard_map/all_to_all | solution.py:152
  372.3 13.7 %copy-start.30 = (f32[96,10]{0,1:T(8,128)S(1)}, f32[96,10]{0,1:T(8,128)}, u32[]{:S(2)}) copy-start(f32[96,10]{0,1:T(8,128)} %param.11) | copy-start | bytes 11524
  372.3 14.8 %copy-start.31 = (f32[96,10]{0,1:T(8,128)S(1)}, f32[96,10]{0,1:T(8,128)}, u32[]{:S(2)}) copy-start(f32[96,10]{0,1:T(8,128)} %param.12) | copy-start | bytes 11524
  372.3 15.9 %copy-start.13 = (f32[2,26,26,10,10]{2,0,4,3,1:T(2,128)S(1)}, f32[2,26,26,10,10]{2,0,4,3,1:T(2,128)}, u32[]{:S(2)}) copy-start(f32[2,26,26,10,10]{2,0,4,3,1:T(2,128)} %param.13) | copy-start | bytes 1622404
  379.4 26.3 %all-to-all-start.1 = ((bf16[8,2,18432]{2,1,0:T(2,128)(2,1)}), bf16[8,2,18432]{2,1,0:T(2,128)(2,1)}, u32[]{:S(2)}, u32[]{:S(2)}) async-start(bf16[8,2,18432]{2,1,0:T(2,128)(2,1)} %reshape.173), calls=%async_computation.1 | async-start | bytes 1179648 | tf_op jit(solution)/shard_map/all_to_all | solution.py:153
  385.3 77.0 %all-reduce.7.cloned.1.call-start = ((), (), s32[]{:S(2)}) async-start(), calls=%async_computation.5 | async-start | bytes 2359296 | tf_op jit(solution)/shard_map/psum | solution.py:160
  405.6 15.4 %copy-start.14 = (bf16[16,2,8,1152]{3,0,2,1:T(8,128)(2,1)}, bf16[16,2,8,1152]{3,0,2,1:T(8,128)(2,1)S(1)}, u32[]{:S(2)}) copy-start(bf16[16,2,8,1152]{3,0,2,1:T(8,128)(2,1)S(1)} %copy.302) | copy-start | bytes 1769476
  411.5 10.5 copy-start.29
  423.1 706.6 %all-reduce.5.cloned.1.call-start = ((), (), s32[]{:S(2)}) async-start(), calls=%async_computation.4 | async-start | bytes 8519680 | tf_op jit(solution)/shard_map/psum | solution.py:166
  470.9 31.1 %copy-start.4 = (f32[2,26,1152]{1,0,2:T(2,128)S(1)}, f32[2,26,1152]{1,0,2:T(2,128)}, u32[]{:S(2)}) copy-start(f32[2,26,1152]{1,0,2:T(2,128)} %copy.220) | copy-start | bytes 718852
  583.0 34.6 %copy-start.8 = (f32[1152,26,26]{0,2,1:T(8,128)S(1)}, f32[1152,26,26]{0,2,1:T(8,128)}, u32[]{:S(2)}) copy-start(f32[1152,26,26]{0,2,1:T(8,128)} %copy.308) | copy-start | bytes 9345028
  583.0 34.6 %copy-start.12 = (f32[1,26,26,10,10]{2,0,4,3,1:T(1,128)S(1)}, f32[1,26,26,10,10]{2,0,4,3,1:T(1,128)}, u32[]{:S(2)}) copy-start(f32[1,26,26,10,10]{2,0,4,3,1:T(1,128)} %get-tuple-element.43) | copy-start | bytes 811204
  583.0 34.6 %copy-start.18 = (f32[1152,10]{0,1:T(8,128)S(1)}, f32[1152,10]{0,1:T(8,128)}, u32[]{:S(2)}) copy-start(f32[1152,10]{0,1:T(8,128)} %fusion.78) | copy-start | bytes 138244
  617.6 36.4 %copy-start.7 = (f32[1,26,26,10,10]{2,0,4,3,1:T(1,128)S(1)}, f32[1,26,26,10,10]{2,0,4,3,1:T(1,128)}, u32[]{:S(2)}) copy-start(f32[1,26,26,10,10]{2,0,4,3,1:T(1,128)} %get-tuple-element.44) | copy-start | bytes 811204
  617.6 36.4 %copy-start.17 = (f32[1152,10]{0,1:T(8,128)S(1)}, f32[1152,10]{0,1:T(8,128)}, u32[]{:S(2)}) copy-start(f32[1152,10]{0,1:T(8,128)} %fusion.77) | copy-start | bytes 138244
  716.5 33.8 %copy-start.2 = (f32[1152,26,26]{2,1,0:T(8,128)S(1)}, f32[1152,26,26]{2,1,0:T(8,128)}, u32[]{:S(2)}) copy-start(f32[1152,26,26]{2,1,0:T(8,128)} %copy.263) | copy-start | bytes 9345028
  781.2 16.0 %copy-start.5 = (f32[2,26,1152]{1,0,2:T(2,128)S(1)}, f32[2,26,1152]{1,0,2:T(2,128)}, u32[]{:S(2)}) copy-start(f32[2,26,1152]{1,0,2:T(2,128)} %copy.220) | copy-start | bytes 718852
  941.5 10.8 copy-start.16
  987.8 33.1 %copy-start.3 = (f32[1152,26,26]{2,1,0:T(8,128)S(1)}, f32[1152,26,26]{2,1,0:T(8,128)}, u32[]{:S(2)}) copy-start(f32[1152,26,26]{2,1,0:T(8,128)} %copy.257) | copy-start | bytes 9345028
  987.8 33.1 %copy-start.11 = (f32[1152,2,26]{2,1,0:T(2,128)S(1)}, f32[1152,2,26]{2,1,0:T(2,128)}, u32[]{:S(2)}) copy-start(f32[1152,2,26]{2,1,0:T(2,128)} %fusion.8) | copy-start | bytes 718852
  1021.0 32.0 %copy-start.15 = (bf16[16,2,8,1152]{3,0,2,1:T(8,128)(2,1)S(1)}, bf16[16,2,8,1152]{3,0,2,1:T(8,128)(2,1)}, u32[]{:S(2)}) copy-start(bf16[16,2,8,1152]{3,0,2,1:T(8,128)(2,1)} %copy-done.14) | copy-start | bytes 1769476
  1051.0 2.5 copy-start.6
  1051.0 2.5 copy-start.10
  1053.6 15.3 %copy-start.9 = (f32[1152,2,26]{2,1,0:T(2,128)S(1)}, f32[1152,2,26]{2,1,0:T(2,128)}, u32[]{:S(2)}) copy-start(f32[1152,2,26]{2,1,0:T(2,128)} %fusion.2) | copy-start | bytes 718852
  1084.3 2.1 copy-start.21
  1084.3 2.1 copy-start.22
  1084.3 2.6 copy-start.23
  1084.4 2.8 copy-start.24
  1089.6 45.9 %copy-start.1 = (bf16[64,26]{0,1:T(8,128)(2,1)S(1)}, bf16[64,26]{0,1:T(8,128)(2,1)}, u32[]{:S(2)}) copy-start(bf16[64,26]{0,1:T(8,128)(2,1)} %param.9) | copy-start | bytes 9988
  (6 other events, 8.2 us)
Sparse Core Ops, SparseCore 0:
  423.3 38.9 all-reduce.6
  955.0 158.8 all-reduce.4
where the time goes:
time: 1150 us; the launch traced here: 1140 us
  matrix products  549 us (48%)
  waiting for transfers between devices  244 us (21%)
  local copies, waits for them, and re-layouts  233 us (20%)
  blocking collectives  40.1 us (3%)
  starting transfers between devices  33.5 us (3%)
  other arithmetic  28.9 us (3%)
  between operations  15.1 us (1%)
    dot_general x20, matrix products, product(): return jnp.einsum(form, *operands, precision=precise)  498 us
    all_to_all x1, waiting for transfers between devices, on_device(): lax.all_to_all(to_rows(flat_input), 'sp', split_axis=0, concat_axis=2, ti...  112 us
    all_to_all x1, waiting for transfers between devices, on_device(): lax.all_to_all(to_rows(flat_cot), 'sp', split_axis=0, concat_axis=2, tile...  93.6 us
    unnamed x71, local copies, waits for them, and re-layouts  62 us
    psum x1, blocking collectives, on_device(): lax.psum((core_part, height_part, width_part, input_part, output_part), '...  40.1 us
    psum x1, waiting for transfers between devices, on_device(): left, right = lax.psum((left, right), 'ch')  37.8 us
    dot_general x2, matrix products, to_rows(): jnp.einsum('nhw,wpl->nphl', field, row_weights, preferred_element_type=jn...  36.5 us
    dot_general x6, local copies, waits for them, and re-layouts, product(): return jnp.einsum(form, *operands, precision=precise)  33.4 us
  transfers between devices with their start and end apart: 6, of which 3 were waited for; matrix products, arithmetic and copies ran while one was open for 23% of the time, Pallas kernels for 0%

commit v1 on v0

v1 whole, which is shorter than its diff:
```python
import functools
import math

import jax
import jax.numpy as jnp
import numpy as np
from jax import lax
from jax.experimental import pallas as pl
from jax.experimental.pallas import tpu as pltpu
from jax.sharding import PartitionSpec as P

f32 = jnp.float32
bf16 = jnp.bfloat16
AXES = ("sp", "ch")
LANE = 128
VMEM_LIMIT = 60 * 1024 * 1024


def round_up(value, unit):
    return -(-value // unit) * unit


def row_tables(batch, width, modes):
    phases = (np.arange(width)[:, None] * np.arange(modes)[None, :] % width).astype(np.float32)
    angles = phases * np.float32(2.0 * math.pi / width)
    scaling = np.float32(1.0 / math.sqrt(width))
    table = np.concatenate([np.cos(angles) * scaling, -np.sin(angles) * scaling], axis=1)
    span = 2 * modes
    reach = max(round_up(b * span % LANE + span, LANE) for b in range(batch))
    full = np.zeros((batch, width, reach), np.float32)
    for b in range(batch):
        full[b, :, b * span % LANE : b * span % LANE + span] = table
    return jnp.asarray(full, dtype=bf16)


class Plan:
    def __init__(self, total, kept):
        bits = total.bit_length() - 1
        self.total = total
        self.halvings = 0
        while self.halvings < bits and kept % (2 << self.halvings) == 0:
            self.halvings += 1
        self.owners = 1 << self.halvings
        self.per = kept // self.owners
        first = list(range(self.halvings))
        second = list(first)
        if self.halvings > 2:
            second[1], second[2] = second[2], second[1]
        self.orders = (first, second)
        self.rest = list(range(self.halvings, bits))

    def flips(self, color):
        order = self.orders[color]
        masks = []
        for relative in range(self.owners):
            mask = 0
            for turn, bit in enumerate(order):
                if relative >> (self.halvings - 1 - turn) & 1:
                    mask |= 1 << bit
            masks.append(mask)
        return np.asarray(masks, dtype=np.int32)

    def swap(self, value, bit):
        pairs = [(i, i ^ (1 << bit)) for i in range(self.total)]
        return lax.ppermute(value, AXES, pairs)


def reduce_scatter(plan, color, keep, send):
    for turn, bit in enumerate(plan.orders[color]):
        total = keep + plan.swap(send, bit).astype(f32)
        if turn + 1 < plan.halvings:
            middle = total.shape[0] // 2
            keep, send = total[:middle], total[middle:].astype(bf16)
    for bit in plan.rest:
        value = total.astype(bf16)
        total = value.astype(f32) + plan.swap(value, bit).astype(f32)
    return total


def all_gather(plan, color, value):
    other = value
    for turn, bit in enumerate(reversed(plan.orders[color])):
        if turn > 0:
            value = jnp.concatenate([value, other], axis=0)
        other = plan.swap(value, bit)
    return value, other


def column_tables(plan, kept, rows_here, height, me, shard):
    owner = me & (plan.owners - 1)
    heights = shard * rows_here + jnp.arange(rows_here, dtype=jnp.int32)
    flips = jnp.asarray(np.stack([plan.flips(0), plan.flips(1)]))
    owned = jnp.bitwise_xor(owner, flips)
    ordinal = jnp.arange(plan.per, dtype=jnp.int32)[None, :, None] * plan.owners + owned[:, None, :]
    ordinal = ordinal.reshape(2, kept)
    frequency = jnp.where(ordinal < kept // 2, ordinal, ordinal + (height - kept))
    phases = (frequency[:, :, None] * heights[None, None, :] % height).astype(f32)
    angles = phases * (2.0 * math.pi / height)
    scaling = 1.0 / math.sqrt(height)
    cosine = (jnp.cos(angles) * scaling).astype(bf16)
    sines = (jnp.sin(angles) * scaling).astype(bf16)
    forth = jnp.concatenate([cosine, sines], axis=1)
    back = jnp.concatenate([jnp.swapaxes(cosine, 1, 2), jnp.swapaxes(sines, 1, 2)], axis=1)
    return forth, back


def turned(value, modes, sign):
    lanes = value.shape[1]
    lane = lax.broadcasted_iota(jnp.int32, value.shape, 1)
    even = (lane // modes) % 2 == 0
    ahead = pltpu.roll(value, lanes - modes, 1)
    behind = pltpu.roll(value, modes, 1)
    if sign > 0:
        return jnp.where(even, ahead, -behind)
    return jnp.where(even, -ahead, behind)


def forward_kernel(
    x_ref, table_ref, factor_ref, forth_ref, rows_ref, keep0_ref, send0_ref, keep1_ref, send1_ref,
    raw, projected, packed, *, plan, rank, rows_here,
):
    step = pl.program_id(0)
    batch, channels, block, width = x_ref.shape
    lanes = keep0_ref.shape[1]
    span = lanes // batch
    modes = span // 2
    tiles = lanes // LANE
    kept = plan.per * plan.owners
    half = rank // 2
    rank_pad = factor_ref.shape[0]
    segment = packed.shape[1] // (2 * plan.owners)
    reach = table_ref.shape[2] // LANE
    for b in range(batch):
        values = jnp.dot(x_ref[b].reshape(channels * block, width), table_ref[b], preferred_element_type=f32)
        for t in range(reach):
            raw[b * reach + t] = values[:, t * LANE : (t + 1) * LANE]
    for h in range(block):
        parts = [None] * tiles
        for b in range(batch):
            for t in range(reach):
                place = b * span // LANE + t
                if place < tiles:
                    piece = raw[b * reach + t, pl.ds(h, channels, stride=block), :]
                    parts[place] = piece if parts[place] is None else parts[place] + piece
        joined = jnp.concatenate(parts, axis=1).astype(bf16)
        rows_ref[:, h * lanes : (h + 1) * lanes] = joined
        mixed = jnp.dot(factor_ref[...], joined, preferred_element_type=f32)
        for t in range(tiles):
            projected[t, pl.ds(step * block + h, rank_pad, stride=rows_here), :] = mixed[:, t * LANE : (t + 1) * LANE]

    @pl.when(step == pl.num_programs(0) - 1)
    def _():
        if segment > plan.per * half:
            for color in range(2):
                for spare in range(plan.per * half, segment):
                    for t in range(tiles):
                        packed[t, pl.ds(color * plan.owners * segment + spare, plan.owners, stride=segment), :] = (
                            jnp.zeros((plan.owners, LANE), f32)
                        )
        for color in range(2):

            @pl.loop(0, half)
            def _(a):
                start = pl.multiple_of((color * half + a) * rows_here, 8)
                plane = jnp.concatenate(
                    [projected[t, pl.ds(start, rows_here), :] for t in range(tiles)], axis=1
                ).astype(bf16)
                both = jnp.dot(forth_ref[color], plane, preferred_element_type=f32)
                spectrum = both[:kept] + turned(both[kept:], modes, 1)
                for j in range(plan.per):
                    for t in range(tiles):
                        packed[
                            t, pl.ds(color * plan.owners * segment + j * half + a, plan.owners, stride=segment), :
                        ] = spectrum[j * plan.owners : (j + 1) * plan.owners, t * LANE : (t + 1) * LANE]

        middle = keep0_ref.shape[0]
        for t in range(tiles):
            for color, (keep_ref, send_ref) in enumerate(((keep0_ref, send0_ref), (keep1_ref, send1_ref))):
                start = 2 * color * middle
                keep_ref[:, t * LANE : (t + 1) * LANE] = packed[t, start : start + middle]
                send_ref[:, t * LANE : (t + 1) * LANE] = packed[t, start + middle : start + 2 * middle].astype(bf16)


def forward(plan, field, table, factor, forth, rank, modes):
    batch, channels, rows_here, width = field.shape
    span = 2 * modes
    lanes = batch * span
    kept = plan.per * plan.owners
    block = min(16, rows_here)
    segment = round_up(plan.per * rank // 2, 8)
    rank_pad = factor.shape[0]
    middle = plan.owners * segment // 2
    return pl.pallas_call(
        functools.partial(forward_kernel, plan=plan, rank=rank, rows_here=rows_here),
        grid=(rows_here // block,),
        in_specs=[
            pl.BlockSpec((batch, channels, block, width), lambda s: (0, 0, s, 0)),
            pl.BlockSpec(table.shape, lambda s: (0, 0, 0)),
            pl.BlockSpec((rank_pad, channels), lambda s: (0, 0)),
            pl.BlockSpec((2, 2 * kept, rows_here), lambda s: (0, 0, 0)),
        ],
        out_specs=[
            pl.BlockSpec((channels, block * lanes), lambda s: (0, s)),
        ]
        + [pl.BlockSpec((middle, lanes), lambda s: (0, 0))] * 4,
        out_shape=[
            jax.ShapeDtypeStruct((channels, rows_here * lanes), bf16),
        ]
        + [jax.ShapeDtypeStruct((middle, lanes), dtype) for dtype in (f32, bf16, f32, bf16)],
        scratch_shapes=[
            pltpu.VMEM((batch * table.shape[2] // LANE, channels * block, LANE), f32),
            pltpu.VMEM((lanes // LANE, rank_pad * rows_here, LANE), f32),
            pltpu.VMEM((lanes // LANE, 2 * plan.owners * segment, LANE), f32),
        ],
        compiler_params=pltpu.CompilerParams(vmem_limit_bytes=VMEM_LIMIT),
        cost_estimate=pl.CostEstimate(
            flops=2 * batch * channels * rows_here * width * span,
            bytes_accessed=2 * batch * channels * rows_here * (width + span),
            transcendentals=0,
        ),
    )(field, table, factor, forth)


def backward_kernel(
    g00_ref, g01_ref, g10_ref, g11_ref, rows_in_ref, rows_out_ref, back_ref, out_in_ref, out_out_ref,
    wide, grids_in, grids_out, block_in, block_out, *, plan, ranks, rows_here, modes,
):
    step = pl.program_id(0)
    tiles = wide.shape[0]
    lanes = tiles * LANE
    segments = [round_up(plan.per * rank // 2, 8) for rank in ranks]
    stride = sum(segments)

    @pl.when(step == 0)
    def _():
        out_in_ref[...] = jnp.zeros_like(out_in_ref)
        out_out_ref[...] = jnp.zeros_like(out_out_ref)
        for grids, rank in zip((grids_in, grids_out), ranks):
            spare = grids.shape[1] - rank * rows_here
            if spare:
                grids[:, rank * rows_here :, :] = jnp.zeros((tiles, spare, LANE), f32)
        for color, (one, other) in enumerate(((g00_ref, g01_ref), (g10_ref, g11_ref))):
            middle = one.shape[0]
            for t in range(tiles):
                wide[t, :middle, :] = one[:, t * LANE : (t + 1) * LANE].astype(f32)
                wide[t, middle:, :] = other[:, t * LANE : (t + 1) * LANE].astype(f32)
            for side, (grids, rank) in enumerate(zip((grids_in, grids_out), ranks)):
                half = rank // 2
                base = side * segments[0]

                @pl.loop(0, half)
                def _(a):
                    spectrum = jnp.concatenate(
                        [
                            jnp.concatenate(
                                [
                                    wide[t, pl.ds(base + j * half + a, plan.owners, stride=stride), :]
                                    for t in range(tiles)
                                ],
                                axis=1,
                            )
                            for j in range(plan.per)
                        ],
                        axis=0,
                    ).astype(bf16)
                    both = jnp.dot(back_ref[color], spectrum, preferred_element_type=f32)
                    start = pl.multiple_of((color * half + a) * rows_here, 8)
                    grid = both[:rows_here] + turned(both[rows_here:], modes, -1)
                    for t in range(tiles):
                        grids[t, pl.ds(start, rows_here), :] = grid[:, t * LANE : (t + 1) * LANE]

    for grids, block_ref, rows_ref, out_ref in (
        (grids_in, block_in, rows_in_ref, out_in_ref),
        (grids_out, block_out, rows_out_ref, out_out_ref),
    ):
        for h in range(block_ref.shape[1] // lanes):
            for t in range(tiles):
                block_ref[:, h * lanes + t * LANE : h * lanes + (t + 1) * LANE] = grids[
                    t, pl.ds(step * (block_ref.shape[1] // lanes) + h, block_ref.shape[0], stride=rows_here), :
                ].astype(bf16)
        out_ref[...] += lax.dot_general(
            rows_ref[...], block_ref[...], (((1,), (1,)), ((), ())), preferred_element_type=f32
        )


def backward(plan, pieces, rows_in, rows_out, back, ranks, rows_here, modes):
    channels = rows_in.shape[0]
    lanes = rows_in.shape[1] // rows_here
    block = min(16, rows_here)
    pads = [round_up(rank, 8) for rank in ranks]
    whole = lambda s: (0, 0)
    part = pl.BlockSpec((channels, block * lanes), lambda s: (0, s))
    return pl.pallas_call(
        functools.partial(backward_kernel, plan=plan, ranks=ranks, rows_here=rows_here, modes=modes),
        grid=(rows_here // block,),
        in_specs=[pl.BlockSpec(piece.shape, whole) for piece in pieces]
        + [part, part, pl.BlockSpec(back.shape, lambda s: (0, 0, 0))],
        out_specs=[pl.BlockSpec((channels, pad), whole) for pad in pads],
        out_shape=[jax.ShapeDtypeStruct((channels, pad), f32) for pad in pads],
        scratch_shapes=[pltpu.VMEM((lanes // LANE, 2 * pieces[0].shape[0], LANE), f32)]
        + [pltpu.VMEM((lanes // LANE, pad * rows_here, LANE), f32) for pad in pads]
        + [pltpu.VMEM((pad, block * lanes), bf16) for pad in pads],
        compiler_params=pltpu.CompilerParams(vmem_limit_bytes=VMEM_LIMIT),
        cost_estimate=pl.CostEstimate(
            flops=2 * channels * sum(pads) * rows_here * lanes,
            bytes_accessed=4 * channels * rows_here * lanes,
            transcendentals=0,
        ),
    )(*pieces, rows_in, rows_out, back)


def owner_kernel(
    left0_ref, left1_ref, right0_ref, right1_ref, core_ref, core_t_ref, modes_ref, height_ref, width_ref,
    core_out, height_out, width_out, back0_ref, back1_ref, modal, pair, pair_low,
    *, plan, batch, rank_in, rank_out, modes,
):
    pad_in, pad_out = round_up(rank_in, 8), round_up(rank_out, 8)
    lanes = left0_ref.shape[1]
    plane = modes_ref.shape[2]
    segment_in = left0_ref.shape[0]
    rows = rank_in * pad_out

    def gathered(refs, j, rank, pad):
        half = rank // 2
        parts = [ref[...].astype(f32)[j * half : (j + 1) * half] for ref in refs]
        if pad > rank:
            parts.append(jnp.zeros((pad - rank, lanes), f32))
        joined = jnp.concatenate(parts, axis=0)
        pieces = []
        for n in range(2 * batch):
            turned_by = (lanes - n * modes) % lanes
            piece = pltpu.roll(joined, turned_by, 1) if turned_by else joined
            pieces.append(piece[:, :plane])
        return pieces

    lane = lax.broadcasted_iota(jnp.int32, (1, plane), 1) < modes

    def spread(pieces):
        total = None
        for n, piece in enumerate(pieces):
            kept = jnp.where(lane, piece, 0.0)
            wide = jnp.concatenate([kept, jnp.zeros((kept.shape[0], lanes - plane), f32)], axis=1)
            wide = pltpu.roll(wide, n * modes, 1) if n else wide
            total = wide if total is None else total + wide
        return total

    core_sum = None
    width_sum = None
    for j in range(plan.per):
        left = gathered((left0_ref, left1_ref), j, rank_in, pad_in)
        right = gathered((right0_ref, right1_ref), j, rank_out, pad_out)
        table = modes_ref[j].astype(bf16)
        table_low = (modes_ref[j] - table.astype(f32)).astype(bf16)
        modal[...] = (
            jnp.dot(core_ref[0], table, preferred_element_type=f32)
            + jnp.dot(core_ref[1], table, preferred_element_type=f32)
            + jnp.dot(core_ref[0], table_low, preferred_element_type=f32)
        )
        inward = [[] for _ in range(2 * batch)]
        outward = [jnp.zeros((pad_out, plane), f32) for _ in range(2 * batch)]
        for a in range(rank_in):
            modal_real = modal[a * pad_out : (a + 1) * pad_out]
            modal_imag = modal[rows + a * pad_out : rows + (a + 1) * pad_out]
            pair_real = jnp.zeros((pad_out, plane), f32)
            pair_imag = jnp.zeros((pad_out, plane), f32)
            for b in range(batch):
                left_real = left[2 * b][a : a + 1]
                left_imag = -left[2 * b + 1][a : a + 1]
                right_real = right[2 * b]
                right_imag = right[2 * b + 1]
                pair_real += left_real * right_real - left_imag * right_imag
                pair_imag += left_real * right_imag + left_imag * right_real
                inward[2 * b].append(
                    jnp.sum(modal_real * right_real + modal_imag * right_imag, axis=0, keepdims=True)
                )
                inward[2 * b + 1].append(
                    jnp.sum(modal_real * right_imag - modal_imag * right_real, axis=0, keepdims=True)
                )
                outward[2 * b] += modal_real * left_real + modal_imag * left_imag
                outward[2 * b + 1] -= modal_real * left_imag - modal_imag * left_real
            for start, value in ((a * pad_out, pair_real), (rows + a * pad_out, pair_imag)):
                high = value.astype(bf16)
                pair[start : start + pad_out] = high
                pair_low[start : start + pad_out] = (value - high.astype(f32)).astype(bf16)
        contract = (((1,), (1,)), ((), ()))
        part = (
            lax.dot_general(pair[...], table, contract, preferred_element_type=f32)
            + lax.dot_general(pair_low[...], table, contract, preferred_element_type=f32)
            + lax.dot_general(pair[...], table_low, contract, preferred_element_type=f32)
        )
        core_sum = part if j == 0 else core_out[...] + part
        core_out[...] = core_sum
        terms = (
            jnp.dot(core_t_ref[0], pair[...], preferred_element_type=f32)
            + jnp.dot(core_t_ref[1], pair[...], preferred_element_type=f32)
            + jnp.dot(core_t_ref[0], pair_low[...], preferred_element_type=f32)
        )
        height_out[j] = jnp.sum(terms * width_ref[...], axis=1, keepdims=True)
        by_width = terms * height_ref[j]
        width_sum = by_width if j == 0 else width_sum + by_width
        half_in, half_out = rank_in // 2, rank_out // 2
        inward_all = spread([jnp.concatenate(rows_of, axis=0) for rows_of in inward])
        outward_all = spread(outward)
        for color, ref in enumerate((back0_ref, back1_ref)):
            ref[j * half_in : (j + 1) * half_in] = inward_all[color * half_in : (color + 1) * half_in]
            ref[segment_in + j * half_out : segment_in + (j + 1) * half_out] = outward_all[
                color * half_out : (color + 1) * half_out
            ]
    for ref in (back0_ref, back1_ref):
        for start, used, stop in (
            (0, plan.per * rank_in // 2, segment_in),
            (segment_in, plan.per * rank_out // 2, ref.shape[0]),
        ):
            if start + used < stop:
                ref[start + used : stop] = jnp.zeros((stop - start - used, lanes), f32)
    width_out[...] = width_sum


def owner_work(plan, left, right, core_tensor, height_rows, width_factor, batch):
    _, rank_in, rank_out, rank_x, rank_y = core_tensor.shape
    modes = width_factor.shape[0]
    pad_out = round_up(rank_out, 8)
    pairs = round_up(rank_x * rank_y, 8)
    plane = round_up(modes, 128)
    lanes = left[0].shape[1]
    rows = left[0].shape[0] + right[0].shape[0]
    spare = pairs - rank_x * rank_y
    core = core_tensor.reshape(2, rank_in, rank_out, rank_x * rank_y)
    core = jnp.pad(core, ((0, 0), (0, 0), (0, pad_out - rank_out), (0, spare)))
    core = core.reshape(2 * rank_in * pad_out, pairs)
    core_high = core.astype(bf16)
    core = jnp.stack([core_high, (core - core_high.astype(f32)).astype(bf16)])
    width_turned = jnp.pad(width_factor.T, ((0, 0), (0, plane - modes)))
    width_wide = jnp.broadcast_to(width_turned[None], (rank_x, rank_y, plane)).reshape(rank_x * rank_y, plane)
    width_wide = jnp.pad(width_wide, ((0, spare), (0, 0)))
    height_wide = jnp.broadcast_to(height_rows[:, :, None], (plan.per, rank_x, rank_y))
    height_wide = jnp.pad(height_wide.reshape(plan.per, rank_x * rank_y, 1), ((0, 0), (0, spare), (0, 0)))
    table = height_wide * width_wide[None]
    core_part, height_part, width_part, back0, back1 = pl.pallas_call(
        functools.partial(
            owner_kernel, plan=plan, batch=batch, rank_in=rank_in, rank_out=rank_out, modes=modes
        ),
        out_shape=[
            jax.ShapeDtypeStruct((2 * rank_in * pad_out, pairs), f32),
            jax.ShapeDtypeStruct((plan.per, pairs, 1), f32),
            jax.ShapeDtypeStruct((pairs, plane), f32),
            jax.ShapeDtypeStruct((rows, lanes), f32),
            jax.ShapeDtypeStruct((rows, lanes), f32),
        ],
        scratch_shapes=[
            pltpu.VMEM((2 * rank_in * pad_out, plane), f32),
            pltpu.VMEM((2 * rank_in * pad_out, plane), bf16),
            pltpu.VMEM((2 * rank_in * pad_out, plane), bf16),
        ],
        compiler_params=pltpu.CompilerParams(vmem_limit_bytes=VMEM_LIMIT),
    )(*left, *right, core, jnp.swapaxes(core, 1, 2), table, height_wide, width_wide)
    height_part = height_part[:, : rank_x * rank_y, 0].reshape(plan.per, rank_x, rank_y).sum(axis=2)
    width_part = width_part[: rank_x * rank_y, :modes].reshape(rank_x, rank_y, modes).sum(axis=0)
    return core_part, height_part, width_part, (back0.astype(bf16), back1.astype(bf16))


def all_reduce(plan, bits, value):
    for bit in bits:
        value = value + plan.swap(value, bit)
    return value


def all_reduce_large(plan, me, value):
    split = []
    for bit in range(plan.total.bit_length() - 1):
        if value.shape[0] % 16 == 0 and len(split) < 3:
            middle = value.shape[0] // 2
            high = (me >> bit) & 1
            keep = lax.dynamic_slice_in_dim(value, high * middle, middle, 0)
            send = lax.dynamic_slice_in_dim(value, (1 - high) * middle, middle, 0).astype(bf16)
            value = keep + plan.swap(send, bit).astype(f32)
            split.append((bit, high))
        else:
            sent = value.astype(bf16)
            value = sent.astype(f32) + plan.swap(sent, bit).astype(f32)
    value = value.astype(bf16)
    for bit, high in reversed(split):
        other = plan.swap(value, bit)
        value = jnp.where(
            high == 0, jnp.concatenate([value, other], axis=0), jnp.concatenate([other, value], axis=0)
        )
    return value.astype(f32)


def on_device(inputs, cotangent, input_factor, output_factor, height_factor, width_factor, core_tensor):
    batch, channels, rows_here, width = inputs.shape
    kept, rank_x = height_factor.shape
    modes, rank_y = width_factor.shape
    rank_in, rank_out = input_factor.shape[1], output_factor.shape[1]
    shards, blocks = lax.axis_size("sp"), lax.axis_size("ch")
    shard = lax.axis_index("sp")
    me = shard * blocks + lax.axis_index("ch")
    plan = Plan(shards * blocks, kept)
    table = row_tables(batch, width, modes)
    forth, back = column_tables(plan, kept, rows_here, rows_here * shards, me, shard)

    def padded(factor):
        rank = factor.shape[1]
        return jnp.pad(factor.T, ((0, round_up(rank, 8) - rank), (0, 0)))

    def scattered(parts):
        return [reduce_scatter(plan, color, parts[2 * color], parts[2 * color + 1]) for color in range(2)]

    rows_input, *left = forward(plan, inputs, table, padded(input_factor), forth, rank_in, modes)
    left = scattered(left)
    rows_cot, *right = forward(plan, cotangent, table, padded(output_factor), forth, rank_out, modes)
    right = scattered(right)

    owner = me & (plan.owners - 1)
    height_rows = height_factor[jnp.arange(plan.per) * plan.owners + owner]
    core_part, height_part, width_part, back_parts = owner_work(
        plan, left, right, core_tensor, height_rows, width_factor, batch
    )
    pieces = []
    for color in range(2):
        pieces.extend(all_gather(plan, color, back_parts[color]))

    counts = (me >> plan.halvings) == 0
    height_full = jnp.zeros((plan.per, plan.owners, rank_x), f32)
    height_full = lax.dynamic_update_slice(height_full, height_part[:, None], (0, owner, 0)).reshape(kept, rank_x)
    small = jnp.concatenate([height_full.T, width_part], axis=0)
    core_rows, core_lanes = core_part.shape
    total_rows = round_up(core_rows + small.shape[0], 64)
    wide_lanes = max(core_lanes, small.shape[1])
    summed = jnp.concatenate(
        [
            jnp.pad(core_part, ((0, 0), (0, wide_lanes - core_lanes))),
            jnp.pad(small, ((0, total_rows - core_rows - small.shape[0]), (0, wide_lanes - small.shape[1]))),
        ],
        axis=0,
    )
    summed = all_reduce_large(plan, me, jnp.where(counts, summed, 0.0))
    core_grad = summed[:core_rows].reshape(2, rank_in, -1, wide_lanes)[:, :, :rank_out, : rank_x * rank_y]
    core_grad = core_grad.reshape(core_tensor.shape)
    height_grad = summed[core_rows : core_rows + rank_x, :kept].T
    width_grad = summed[core_rows + rank_x : core_rows + rank_x + rank_y, :modes].T

    input_part, output_part = backward(
        plan, pieces, rows_input, rows_cot, back, (rank_in, rank_out), rows_here, modes
    )
    input_part, output_part = input_part[:, :rank_in], output_part[:, :rank_out]
    over_rows = range(blocks.bit_length() - 1, plan.total.bit_length() - 1)
    both = all_reduce(plan, over_rows, jnp.concatenate([input_part, output_part], axis=0))
    return (core_grad, both[:channels], both[channels:], height_grad, width_grad)


def solution(mesh):
    placed = (
        P(None, "ch", "sp", None),
        P(None, "ch", "sp", None),
        P("ch", None),
        P("ch", None),
        P(),
        P(),
        P(),
    )
    return jax.shard_map(
        on_device,
        mesh=mesh,
        in_specs=placed,
        out_specs=(P(), P("ch", None), P("ch", None), P(), P()),
        check_vma=False,
    )
```

time: 1150 us -> 232 us (0.20)
  matrix products: 549 us -> 0 us
  local copies, waits for them, and re-layouts: 233 us -> 18.4 us
  waiting for transfers between devices: 244 us -> 44.2 us
  Pallas kernels: 0 us -> 109 us
  blocking collectives: 40.1 us -> 0 us
  between operations: 15.1 us -> 1.25 us
  other arithmetic: 28.9 us -> 16.5 us
    dot_general x30 -> x0, matrix products: 549 us -> none  [the longest x20 498 us: product(): return jnp.einsum(form, *operands, precision=precise)]
    all_to_all x4 -> x0, waiting for transfers between devices: 206 us -> none  [the longest x1 112 us: on_device(): lax.all_to_all(to_rows(flat_input), 'sp', split_axis=0, concat_axis=2, ti...]
    pallas_call x0 -> x4, Pallas kernels: none -> 109 us  [the longest x2 66.8 us: forward(): pl.pallas_call(functools.partial(forward_kernel, plan=plan, rank=rank, ro...]
    unnamed x71 -> x27, local copies, waits for them, and re-layouts: 62 us -> 1.22 us
    ppermute x0 -> x41, waiting for transfers between devices: none -> 44.2 us  [swap(): return lax.ppermute(value, AXES, pairs)]
    ppermute x0 -> x41, starting transfers between devices: none -> 42.6 us  [swap(): return lax.ppermute(value, AXES, pairs)]
    all_to_all x4 -> x0, local copies, waits for them, and re-layouts: 40.2 us -> none  [the longest x1 10.7 us: on_device(): lax.all_to_all(to_rows(flat_input), 'sp', split_axis=0, concat_axis=2, ti...]
    psum x1 -> x0, blocking collectives: 40.1 us -> none  [on_device(): lax.psum((core_part, height_part, width_part, input_part, output_part), '...]
  transfers between devices with their start and end apart: 6 -> 41, of which waited for: 3 -> 19; matrix products, arithmetic and copies ran while one was open for 23% -> 12% of each run, Pallas kernels for 0% -> 29%
where the time goes in v1:
time: 232 us
  Pallas kernels  109 us (47%)
  waiting for transfers between devices  44.2 us (19%)
  starting transfers between devices  42.6 us (18%)
  local copies, waits for them, and re-layouts  18.4 us (8%)
  other arithmetic  16.5 us (7%)
    pallas_call x2, Pallas kernels, forward(): pl.pallas_call(functools.partial(forward_kernel, plan=plan, rank=rank, ro...  66.8 us
    ppermute x41, waiting for transfers between devices, swap(): return lax.ppermute(value, AXES, pairs)  44.2 us
    ppermute x41, starting transfers between devices, swap(): return lax.ppermute(value, AXES, pairs)  42.6 us
    pallas_call x1, Pallas kernels, backward(): pl.pallas_call(functools.partial(backward_kernel, plan=plan, ranks=ranks,...  34.6 us
    pallas_call x1, Pallas kernels, owner_work(): pl.pallas_call(functools.partial(owner_kernel, plan=plan, batch=batch, ra...  7.36 us
    add x20, other arithmetic, reduce_scatter(): total = keep + plan.swap(send, bit).astype(f32)  6.63 us
  transfers between devices with their start and end apart: 41, of which 19 were waited for; matrix products, arithmetic and copies ran while one was open for 12% of the time, Pallas kernels for 29%

profile of v1, /device:TPU:0, one launch (start us, length us, event | category | flops | bytes accessed | tf_op | source)
XLA Modules:
  0.0 231.7 jit_solution(137400731273984461)
XLA Ops:
  4.0 33.4 %shard_map.129 = (bf16[64,49152]{1,0:T(8,128)(2,1)}, f32[640,384]{1,0:T(8,128)}, bf16[640,384]{1,0:T(8,128)(2,1)}, f32[640,384]{1,0:T(8,128)}, bf16[640,384]{1,0:T(8,128)(2,1)}) custom-call(bf16[2,64,128,1024]{3,2,1,0:T(8,128)(2,1)} %x_ref.3, bf16[2,1024,256]{2,1,0:T(8,128)(2,1)} %constant.72.clone.table_ref, bf16[32,64]{1,0:T(8,128)(2,1)} %pad.28.factor_ref, ...), custom_call_target="tpu_custom_call" | custom-call | flops 6442450944 | bytes 39845888 | tf_op jit(solution)/shard_map/pallas_call | solution.py:193
  38.6 33.4 %shard_map.128 = (bf16[64,49152]{1,0:T(8,128)(2,1)}, f32[640,384]{1,0:T(8,128)}, bf16[640,384]{1,0:T(8,128)(2,1)}, f32[640,384]{1,0:T(8,128)}, bf16[640,384]{1,0:T(8,128)(2,1)}) custom-call(bf16[2,64,128,1024]{3,2,1,0:T(8,128)(2,1)} %x_ref.2, bf16[2,1024,256]{2,1,0:T(8,128)(2,1)} %constant.72.clone.table_ref, bf16[32,64]{1,0:T(8,128)(2,1)} %pad.27.factor_ref, ...), custom_call_target="tpu_custom_call" | custom-call | flops 6442450944 | bytes 39845888 | tf_op jit(solution)/shard_map/pallas_call | solution.py:193
  73.5 3.5 %copy.31 = f32[2,26,26,100]{3,2,1,0:T(8,128)S(1)} copy(f32[2,26,26,100]{2,0,3,1:T(2,128)} %bitcast.25) | data formatting | bytes 1081600 | tf_op jit(solution)/shard_map/reshape | solution.py:428
  82.5 3.0 %collective-permute-start.16 = (bf16[320,384]{1,0:T(8,128)(2,1)S(1)}, bf16[320,384]{1,0:T(8,128)(2,1)S(1)}, u32[]{:S(2)}, u32[]{:S(2)}) collective-permute-start(bf16[320,384]{1,0:T(8,128)(2,1)S(1)} %slice.259), channel_id=1, source_target_pairs={{0,4},{1,5},{2,6},{3,7},{4,0},{5,1},{6,2},{7,3},{8,12},{9,13},{10,... | collective-permute-start | bytes 737288 | tf_op jit(solution)/shard_map/ppermute | solution.py:65
  90.3 1.6 collective-permute-done.16
  92.0 2.5 %collective-permute-start.17 = (bf16[160,384]{1,0:T(8,128)(2,1)S(1)}, bf16[160,384]{1,0:T(8,128)(2,1)S(1)}, u32[]{:S(2)}, u32[]{:S(2)}) collective-permute-start(bf16[160,384]{1,0:T(8,128)(2,1)S(1)} %slice.263), channel_id=1, source_target_pairs={{0,2},{1,3},{2,0},{3,1},{4,6},{5,7},{6,4},{7,5},{8,10},{9,11},{10,... | collective-permute-start | bytes 368648 | tf_op jit(solution)/shard_map/ppermute | solution.py:65
  96.1 1.8 collective-permute-done.6
  98.0 1.8 collective-permute-start.7
  101.4 2.1 collective-permute-done.17
  103.5 1.6 collective-permute-start.18
  105.8 1.6 collective-permute-start.8
  108.0 2.7 %collective-permute-start.19 = (bf16[40,384]{1,0:T(8,128)(2,1)S(1)}, bf16[40,384]{1,0:T(8,128)(2,1)S(1)}, u32[]{:S(2)}, u32[]{:S(2)}) collective-permute-start(bf16[40,384]{1,0:T(8,128)(2,1)S(1)} %slice.271), channel_id=1, source_target_pairs={{0,16},{1,17},{2,18},{3,19},{4,20},{5,21},{6,22},{7,23},{8,24},{9,... | collective-permute-start | bytes 92168 | tf_op jit(solution)/shard_map/ppermute | solution.py:65
  110.7 1.6 collective-permute-start.14
  113.9 1.6 collective-permute-start.4
  119.4 7.4 %shard_map.130 = (f32[1664,104]{1,0:T(8,128)}, f32[3,104,1]{2,1,0:T(8,128)}, f32[104,128]{1,0:T(8,128)}, f32[80,384]{1,0:T(8,128)}, f32[80,384]{1,0:T(8,128)}) custom-call(f32[40,384]{1,0:T(8,128)} %slice_add_fusion.15.left0_ref, f32[40,384]{1,0:T(8,128)} %slice_add_fusion.14.left1_ref, f32[40,384]{1,0:T(8,128)} %slice_add_fusion.13.right0_ref, ...), custom_call_target="tpu_custom_call" | custom-call | tf_op jit(solution)/shard_map/pallas_call | solution.py:439
  127.6 1.6 collective-permute-start.33
  135.4 2.8 %collective-permute-start.34 = (bf16[160,384]{1,0:T(8,128)(2,1)S(1)}, bf16[160,384]{1,0:T(8,128)(2,1)S(1)}, u32[]{:S(2)}, u32[]{:S(2)}) collective-permute-start(bf16[160,384]{1,0:T(8,128)(2,1)S(1)} %pad_maximum_fusion.7), channel_id=1, source_target_pairs={{0,8},{1,9},{2,10},{3,11},{4,12},{5,13},{6,14},{7,15},{8,0},{9,1},... | collective-permute-start | bytes 368648 | tf_op jit(solution)/shard_map/ppermute | solution.py:65
  138.4 1.6 collective-permute-start.21
  140.0 2.4 %collective-permute-done.34 = bf16[160,384]{1,0:T(8,128)(2,1)S(1)} collective-permute-done((bf16[160,384]{1,0:T(8,128)(2,1)S(1)}, bf16[160,384]{1,0:T(8,128)(2,1)S(1)}, u32[]{:S(2)}, u32[]{:S(2)}) %collective-permute-start.34) | collective-permute-done | bytes 122912 | tf_op jit(solution)/shard_map/ppermute | solution.py:65
  145.5 1.6 collective-permute-start.22
  147.1 2.9 %collective-permute-done.35 = bf16[320,384]{1,0:T(8,128)(2,1)S(1)} collective-permute-done((bf16[320,384]{1,0:T(8,128)(2,1)S(1)}, bf16[320,384]{1,0:T(8,128)(2,1)S(1)}, u32[]{:S(2)}, u32[]{:S(2)}) %collective-permute-start.35) | collective-permute-done | bytes 245792 | tf_op jit(solution)/shard_map/ppermute | solution.py:65
  150.7 3.1 %collective-permute-done.30 = bf16[320,384]{1,0:T(8,128)(2,1)S(1)} collective-permute-done((bf16[320,384]{1,0:T(8,128)(2,1)S(1)}, bf16[320,384]{1,0:T(8,128)(2,1)S(1)}, u32[]{:S(2)}, u32[]{:S(2)}) %collective-permute-start.30) | collective-permute-done | bytes 245792 | tf_op jit(solution)/shard_map/ppermute | solution.py:65
  153.8 1.6 collective-permute-start.31
  155.4 1.8 collective-permute-start.23
  157.3 7.1 %collective-permute-done.36 = bf16[640,384]{1,0:T(8,128)(2,1)S(1)} collective-permute-done((bf16[640,384]{1,0:T(8,128)(2,1)S(1)}, bf16[640,384]{1,0:T(8,128)(2,1)S(1)}, u32[]{:S(2)}, u32[]{:S(2)}) %collective-permute-start.36) | collective-permute-done | bytes 491552 | tf_op jit(solution)/shard_map/ppermute | solution.py:65
  166.3 5.3 %collective-permute-done.24 = bf16[216,104]{1,0:T(8,128)(2,1)S(1)} collective-permute-done((bf16[216,104]{1,0:T(8,128)(2,1)S(1)}, bf16[216,104]{1,0:T(8,128)(2,1)S(1)}, u32[]{:S(2)}, u32[]{:S(2)}) %collective-permute-start.24) | collective-permute-done | bytes 44960 | tf_op jit(solution)/shard_map/ppermute | solution.py:65
  172.2 3.6 %collective-permute-done.25 = bf16[216,104]{1,0:T(8,128)(2,1)S(1)} collective-permute-done((bf16[216,104]{1,0:T(8,128)(2,1)S(1)}, bf16[216,104]{1,0:T(8,128)(2,1)S(1)}, u32[]{:S(2)}, u32[]{:S(2)}) %collective-permute-start.25) | collective-permute-done | bytes 44960 | tf_op jit(solution)/shard_map/ppermute | solution.py:65
  178.0 2.6 %collective-permute-done.26 = bf16[432,104]{1,0:T(8,128)(2,1)S(1)} collective-permute-done((bf16[432,104]{1,0:T(8,128)(2,1)S(1)}, bf16[432,104]{1,0:T(8,128)(2,1)S(1)}, u32[]{:S(2)}, u32[]{:S(2)}) %collective-permute-start.26) | collective-permute-done | bytes 89888 | tf_op jit(solution)/shard_map/ppermute | solution.py:65
  182.5 34.6 %shard_map.131 = (f32[64,32]{1,0:T(8,128)}, f32[64,32]{1,0:T(8,128)}) custom-call(bf16[1280,384]{1,0:T(8,128)(2,1)} %copy-done.1, bf16[1280,384]{1,0:T(8,128)(2,1)} %collective-permute-done.32.g01_ref, bf16[1280,384]{1,0:T(8,128)(2,1)} %copy-done, bf16[1280,384]{1,0:T(8,128)(2,1)} %copy-done.5, bf16[64,49152]{1,0:T(8,128)(2,1)} %get-tuple-element.35.rows_in_ref, ...), custom_call_target="tpu_custom_call" | custom-call | flops 402653184 | bytes 12582912 | tf_op jit(solution)/shard_map/pallas_call | solution.py:293
  219.4 3.2 %collective-permute-done.38 = f32[128,26]{0,1:T(8,128)S(1)} collective-permute-done((f32[128,26]{0,1:T(8,128)S(1)}, f32[128,26]{0,1:T(8,128)S(1)}, u32[]{:S(2)}, u32[]{:S(2)}) %collective-permute-start.38) | collective-permute-done | bytes 13344 | tf_op jit(solution)/shard_map/ppermute | solution.py:65
  224.1 2.3 collective-permute-done.39
  227.0 2.8 %copy.38 = f32[2,26,26,100]{2,0,3,1:T(2,128)} copy(f32[2,26,26,100]{3,2,1,0:T(8,128)S(1)} %bitcast.24) | data formatting | bytes 1081600 | tf_op jit(solution)/shard_map/slice | solution.py:538
  (190 shorter events, 50.0 us)
Async XLA Ops:
  37.5 43.6 %collective-permute-start.15 = (bf16[640,384]{1,0:T(8,128)(2,1)}, bf16[640,384]{1,0:T(8,128)(2,1)}, u32[]{:S(2)}, u32[]{:S(2)}) collective-permute-start(bf16[640,384]{1,0:T(8,128)(2,1)} %get-tuple-element.29), channel_id=1, source_target_pairs={{0,1},{1,0},{2,3},{3,2},{4,5},{5,4},{6,7},{7,6},{8,9},{9,8},{10,11... | collective-permute-start | bytes 1474568 | tf_op jit(solution)/shard_map/ppermute | solution.py:65
  38.0 47.6 %collective-permute-start.10 = (bf16[640,384]{1,0:T(8,128)(2,1)}, bf16[640,384]{1,0:T(8,128)(2,1)}, u32[]{:S(2)}, u32[]{:S(2)}) collective-permute-start(bf16[640,384]{1,0:T(8,128)(2,1)} %get-tuple-element.27), channel_id=1, source_target_pairs={{0,1},{1,0},{2,3},{3,2},{4,5},{5,4},{6,7},{7,6},{8,9},{9,8},{10,11... | collective-permute-start | bytes 1474568 | tf_op jit(solution)/shard_map/ppermute | solution.py:65
  72.0 16.2 %collective-permute-start.5 = (bf16[640,384]{1,0:T(8,128)(2,1)}, bf16[640,384]{1,0:T(8,128)(2,1)}, u32[]{:S(2)}, u32[]{:S(2)}) collective-permute-start(bf16[640,384]{1,0:T(8,128)(2,1)} %get-tuple-element.25), channel_id=1, source_target_pairs={{0,1},{1,0},{2,3},{3,2},{4,5},{5,4},{6,7},{7,6},{8,9},{9,8},{10,11... | collective-permute-start | bytes 1474568 | tf_op jit(solution)/shard_map/ppermute | solution.py:65
  72.4 17.5 %collective-permute-start = (bf16[640,384]{1,0:T(8,128)(2,1)}, bf16[640,384]{1,0:T(8,128)(2,1)S(1)}, u32[]{:S(2)}, u32[]{:S(2)}) collective-permute-start(bf16[640,384]{1,0:T(8,128)(2,1)} %get-tuple-element.23), channel_id=1, source_target_pairs={{0,1},{1,0},{2,3},{3,2},{4,5},{5,4},{6,7},{7,6},{8,9},{9,8},{10,11... | collective-permute-start | bytes 1474568 | tf_op jit(solution)/shard_map/ppermute | solution.py:65
  82.5 9.4 %collective-permute-start.16 = (bf16[320,384]{1,0:T(8,128)(2,1)S(1)}, bf16[320,384]{1,0:T(8,128)(2,1)S(1)}, u32[]{:S(2)}, u32[]{:S(2)}) collective-permute-start(bf16[320,384]{1,0:T(8,128)(2,1)S(1)} %slice.259), channel_id=1, source_target_pairs={{0,4},{1,5},{2,6},{3,7},{4,0},{5,1},{6,2},{7,3},{8,12},{9,13},{10,... | collective-permute-start | bytes 737288 | tf_op jit(solution)/shard_map/ppermute | solution.py:65
  86.7 8.9 %collective-permute-start.11 = (bf16[320,384]{1,0:T(8,128)(2,1)S(1)}, bf16[320,384]{1,0:T(8,128)(2,1)S(1)}, u32[]{:S(2)}, u32[]{:S(2)}) collective-permute-start(bf16[320,384]{1,0:T(8,128)(2,1)S(1)} %slice.260), channel_id=1, source_target_pairs={{0,2},{1,3},{2,0},{3,1},{4,6},{5,7},{6,4},{7,5},{8,10},{9,11},{10,... | collective-permute-start | bytes 737288 | tf_op jit(solution)/shard_map/ppermute | solution.py:65
  89.4 8.5 %collective-permute-start.6 = (bf16[320,384]{1,0:T(8,128)(2,1)S(1)}, bf16[320,384]{1,0:T(8,128)(2,1)S(1)}, u32[]{:S(2)}, u32[]{:S(2)}) collective-permute-start(bf16[320,384]{1,0:T(8,128)(2,1)S(1)} %slice.261), channel_id=1, source_target_pairs={{0,4},{1,5},{2,6},{3,7},{4,0},{5,1},{6,2},{7,3},{8,12},{9,13},{10,... | collective-permute-start | bytes 737288 | tf_op jit(solution)/shard_map/ppermute | solution.py:65
  90.1 10.7 %collective-permute-start.1 = (bf16[320,384]{1,0:T(8,128)(2,1)S(1)}, bf16[320,384]{1,0:T(8,128)(2,1)S(1)}, u32[]{:S(2)}, u32[]{:S(2)}) collective-permute-start(bf16[320,384]{1,0:T(8,128)(2,1)S(1)} %slice.262), channel_id=1, source_target_pairs={{0,2},{1,3},{2,0},{3,1},{4,6},{5,7},{6,4},{7,5},{8,10},{9,11},{10,... | collective-permute-start | bytes 737288 | tf_op jit(solution)/shard_map/ppermute | solution.py:65
  92.0 11.5 %collective-permute-start.17 = (bf16[160,384]{1,0:T(8,128)(2,1)S(1)}, bf16[160,384]{1,0:T(8,128)(2,1)S(1)}, u32[]{:S(2)}, u32[]{:S(2)}) collective-permute-start(bf16[160,384]{1,0:T(8,128)(2,1)S(1)} %slice.263), channel_id=1, source_target_pairs={{0,2},{1,3},{2,0},{3,1},{4,6},{5,7},{6,4},{7,5},{8,10},{9,11},{10,... | collective-permute-start | bytes 368648 | tf_op jit(solution)/shard_map/ppermute | solution.py:65
  95.7 9.5 %collective-permute-start.12 = (bf16[160,384]{1,0:T(8,128)(2,1)S(1)}, bf16[160,384]{1,0:T(8,128)(2,1)S(1)}, u32[]{:S(2)}, u32[]{:S(2)}) collective-permute-start(bf16[160,384]{1,0:T(8,128)(2,1)S(1)} %slice.264), channel_id=1, source_target_pairs={{0,4},{1,5},{2,6},{3,7},{4,0},{5,1},{6,2},{7,3},{8,12},{9,13},{10,... | collective-permute-start | bytes 368648 | tf_op jit(solution)/shard_map/ppermute | solution.py:65
  98.0 7.8 %collective-permute-start.7 = (bf16[160,384]{1,0:T(8,128)(2,1)S(1)}, bf16[160,384]{1,0:T(8,128)(2,1)S(1)}, u32[]{:S(2)}, u32[]{:S(2)}) collective-permute-start(bf16[160,384]{1,0:T(8,128)(2,1)S(1)} %slice.265), channel_id=1, source_target_pairs={{0,2},{1,3},{2,0},{3,1},{4,6},{5,7},{6,4},{7,5},{8,10},{9,11},{10,... | collective-permute-start | bytes 368648 | tf_op jit(solution)/shard_map/ppermute | solution.py:65
  100.9 6.5 %collective-permute-start.2 = (bf16[160,384]{1,0:T(8,128)(2,1)S(1)}, bf16[160,384]{1,0:T(8,128)(2,1)S(1)}, u32[]{:S(2)}, u32[]{:S(2)}) collective-permute-start(bf16[160,384]{1,0:T(8,128)(2,1)S(1)} %slice.266), channel_id=1, source_target_pairs={{0,4},{1,5},{2,6},{3,7},{4,0},{5,1},{6,2},{7,3},{8,12},{9,13},{10,... | collective-permute-start | bytes 368648 | tf_op jit(solution)/shard_map/ppermute | solution.py:65
  105.2 5.5 %collective-permute-start.13 = (bf16[80,384]{1,0:T(8,128)(2,1)S(1)}, bf16[80,384]{1,0:T(8,128)(2,1)S(1)}, u32[]{:S(2)}, u32[]{:S(2)}) collective-permute-start(bf16[80,384]{1,0:T(8,128)(2,1)S(1)} %slice.268), channel_id=1, source_target_pairs={{0,8},{1,9},{2,10},{3,11},{4,12},{5,13},{6,14},{7,15},{8,0},{9,1},... | collective-permute-start | bytes 184328 | tf_op jit(solution)/shard_map/ppermute | solution.py:65
  105.8 6.5 %collective-permute-start.8 = (bf16[80,384]{1,0:T(8,128)(2,1)S(1)}, bf16[80,384]{1,0:T(8,128)(2,1)S(1)}, u32[]{:S(2)}, u32[]{:S(2)}) collective-permute-start(bf16[80,384]{1,0:T(8,128)(2,1)S(1)} %slice.269), channel_id=1, source_target_pairs={{0,8},{1,9},{2,10},{3,11},{4,12},{5,13},{6,14},{7,15},{8,0},{9,1},... | collective-permute-start | bytes 184328 | tf_op jit(solution)/shard_map/ppermute | solution.py:65
  107.5 6.3 %collective-permute-start.3 = (bf16[80,384]{1,0:T(8,128)(2,1)S(1)}, bf16[80,384]{1,0:T(8,128)(2,1)S(1)}, u32[]{:S(2)}, u32[]{:S(2)}) collective-permute-start(bf16[80,384]{1,0:T(8,128)(2,1)S(1)} %slice.270), channel_id=1, source_target_pairs={{0,8},{1,9},{2,10},{3,11},{4,12},{5,13},{6,14},{7,15},{8,0},{9,1},... | collective-permute-start | bytes 184328 | tf_op jit(solution)/shard_map/ppermute | solution.py:65
  108.0 7.4 %collective-permute-start.19 = (bf16[40,384]{1,0:T(8,128)(2,1)S(1)}, bf16[40,384]{1,0:T(8,128)(2,1)S(1)}, u32[]{:S(2)}, u32[]{:S(2)}) collective-permute-start(bf16[40,384]{1,0:T(8,128)(2,1)S(1)} %slice.271), channel_id=1, source_target_pairs={{0,16},{1,17},{2,18},{3,19},{4,20},{5,21},{6,22},{7,23},{8,24},{9,... | collective-permute-start | bytes 92168 | tf_op jit(solution)/shard_map/ppermute | solution.py:65
  110.7 5.4 %collective-permute-start.14 = (bf16[40,384]{1,0:T(8,128)(2,1)S(1)}, bf16[40,384]{1,0:T(8,128)(2,1)S(1)}, u32[]{:S(2)}, u32[]{:S(2)}) collective-permute-start(bf16[40,384]{1,0:T(8,128)(2,1)S(1)} %slice.272), channel_id=1, source_target_pairs={{0,16},{1,17},{2,18},{3,19},{4,20},{5,21},{6,22},{7,23},{8,24},{9,... | collective-permute-start | bytes 92168 | tf_op jit(solution)/shard_map/ppermute | solution.py:65
  127.6 7.7 %collective-permute-start.33 = (bf16[80,384]{1,0:T(8,128)(2,1)S(1)}, bf16[80,384]{1,0:T(8,128)(2,1)S(1)}, u32[]{:S(2)}, u32[]{:S(2)}) collective-permute-start(bf16[80,384]{1,0:T(8,128)(2,1)S(1)} %get-tuple-element.50), channel_id=1, source_target_pairs={{0,16},{1,17},{2,18},{3,19},{4,20},{5,21},{6,22},{7,23},{8,24},{9,... | collective-permute-start | bytes 184328 | tf_op jit(solution)/shard_map/ppermute | solution.py:65
  130.2 8.0 %collective-permute-start.28 = (bf16[80,384]{1,0:T(8,128)(2,1)S(1)}, bf16[80,384]{1,0:T(8,128)(2,1)S(1)}, u32[]{:S(2)}, u32[]{:S(2)}) collective-permute-start(bf16[80,384]{1,0:T(8,128)(2,1)S(1)} %get-tuple-element.52), channel_id=1, source_target_pairs={{0,16},{1,17},{2,18},{3,19},{4,20},{5,21},{6,22},{7,23},{8,24},{9,... | collective-permute-start | bytes 184328 | tf_op jit(solution)/shard_map/ppermute | solution.py:65
  135.4 7.0 %collective-permute-start.34 = (bf16[160,384]{1,0:T(8,128)(2,1)S(1)}, bf16[160,384]{1,0:T(8,128)(2,1)S(1)}, u32[]{:S(2)}, u32[]{:S(2)}) collective-permute-start(bf16[160,384]{1,0:T(8,128)(2,1)S(1)} %pad_maximum_fusion.7), channel_id=1, source_target_pairs={{0,8},{1,9},{2,10},{3,11},{4,12},{5,13},{6,14},{7,15},{8,0},{9,1},... | collective-permute-start | bytes 368648 | tf_op jit(solution)/shard_map/ppermute | solution.py:65
  138.2 6.6 %collective-permute-start.29 = (bf16[160,384]{1,0:T(8,128)(2,1)S(1)}, bf16[160,384]{1,0:T(8,128)(2,1)S(1)}, u32[]{:S(2)}, u32[]{:S(2)}) collective-permute-start(bf16[160,384]{1,0:T(8,128)(2,1)S(1)} %pad_maximum_fusion.6), channel_id=1, source_target_pairs={{0,8},{1,9},{2,10},{3,11},{4,12},{5,13},{6,14},{7,15},{8,0},{9,1},... | collective-permute-start | bytes 368648 | tf_op jit(solution)/shard_map/ppermute | solution.py:65
  138.4 7.0 %collective-permute-start.21 = (bf16[432,104]{1,0:T(8,128)(2,1)S(1)}, bf16[432,104]{1,0:T(8,128)(2,1)S(1)}, u32[]{:S(2)}, u32[]{:S(2)}) collective-permute-start(bf16[432,104]{1,0:T(8,128)(2,1)S(1)} %dynamic-slice_convert_fusion.1), channel_id=1, source_target_pairs={{0,2},{1,3},{2,0},{3,1},{4,6},{5,7},{6,4},{7,5},{8,10},{9,11},{10,... | collective-permute-start | bytes 269576 | tf_op jit(solution)/shard_map/ppermute | solution.py:65
  142.4 7.6 %collective-permute-start.35 = (bf16[320,384]{1,0:T(8,128)(2,1)S(1)}, bf16[320,384]{1,0:T(8,128)(2,1)S(1)}, u32[]{:S(2)}, u32[]{:S(2)}) collective-permute-start(bf16[320,384]{1,0:T(8,128)(2,1)S(1)} %pad_maximum_fusion.4), channel_id=1, source_target_pairs={{0,2},{1,3},{2,0},{3,1},{4,6},{5,7},{6,4},{7,5},{8,10},{9,11},{10,... | collective-permute-start | bytes 737288 | tf_op jit(solution)/shard_map/ppermute | solution.py:65
  144.8 8.9 %collective-permute-start.30 = (bf16[320,384]{1,0:T(8,128)(2,1)S(1)}, bf16[320,384]{1,0:T(8,128)(2,1)S(1)}, u32[]{:S(2)}, u32[]{:S(2)}) collective-permute-start(bf16[320,384]{1,0:T(8,128)(2,1)S(1)} %pad_maximum_fusion.3), channel_id=1, source_target_pairs={{0,4},{1,5},{2,6},{3,7},{4,0},{5,1},{6,2},{7,3},{8,12},{9,13},{10,... | collective-permute-start | bytes 737288 | tf_op jit(solution)/shard_map/ppermute | solution.py:65
  145.5 9.8 %collective-permute-start.22 = (bf16[216,104]{1,0:T(8,128)(2,1)S(1)}, bf16[216,104]{1,0:T(8,128)(2,1)S(1)}, u32[]{:S(2)}, u32[]{:S(2)}) collective-permute-start(bf16[216,104]{1,0:T(8,128)(2,1)S(1)} %dynamic-slice_convert_fusion.2), channel_id=1, source_target_pairs={{0,4},{1,5},{2,6},{3,7},{4,0},{5,1},{6,2},{7,3},{8,12},{9,13},{10,... | collective-permute-start | bytes 134792 | tf_op jit(solution)/shard_map/ppermute | solution.py:65
  150.1 14.3 %collective-permute-start.36 = (bf16[640,384]{1,0:T(8,128)(2,1)S(1)}, bf16[640,384]{1,0:T(8,128)(2,1)S(1)}, u32[]{:S(2)}, u32[]{:S(2)}) collective-permute-start(bf16[640,384]{1,0:T(8,128)(2,1)S(1)} %pad_maximum_fusion.2), channel_id=1, source_target_pairs={{0,4},{1,5},{2,6},{3,7},{4,0},{5,1},{6,2},{7,3},{8,12},{9,13},{10,... | collective-permute-start | bytes 1474568 | tf_op jit(solution)/shard_map/ppermute | solution.py:65
  153.8 11.2 %collective-permute-start.31 = (bf16[640,384]{1,0:T(8,128)(2,1)S(1)}, bf16[640,384]{1,0:T(8,128)(2,1)S(1)}, u32[]{:S(2)}, u32[]{:S(2)}) collective-permute-start(bf16[640,384]{1,0:T(8,128)(2,1)S(1)} %pad_maximum_fusion.1), channel_id=1, source_target_pairs={{0,2},{1,3},{2,0},{3,1},{4,6},{5,7},{6,4},{7,5},{8,10},{9,11},{10,... | collective-permute-start | bytes 1474568 | tf_op jit(solution)/shard_map/ppermute | solution.py:65
  155.4 9.9 %collective-permute-start.23 = (bf16[216,104]{1,0:T(8,128)(2,1)S(1)}, bf16[216,104]{1,0:T(8,128)(2,1)S(1)}, u32[]{:S(2)}, u32[]{:S(2)}) collective-permute-start(bf16[216,104]{1,0:T(8,128)(2,1)S(1)} %add_convert_fusion.2), channel_id=1, source_target_pairs={{0,8},{1,9},{2,10},{3,11},{4,12},{5,13},{6,14},{7,15},{8,0},{9,1},... | collective-permute-start | bytes 134792 | tf_op jit(solution)/shard_map/ppermute | solution.py:65
  164.5 17.1 %collective-permute-start.37 = (bf16[1280,384]{1,0:T(8,128)(2,1)S(1)}, bf16[1280,384]{1,0:T(8,128)(2,1)S(1)}, u32[]{:S(2)}, u32[]{:S(2)}) collective-permute-start(bf16[1280,384]{1,0:T(8,128)(2,1)S(1)} %constant_dynamic-update-slice_fusion.5.g10_ref), channel_id=1, source_target_pairs={{0,1},{1,0},{2,3},{3,2},{4,5},{5,4},{6,7},{7,6},{8,9},{9,8},{10,11... | collective-permute-start | bytes 2949128 | tf_op jit(solution)/shard_map/ppermute | solution.py:65
  165.1 16.5 %collective-permute-start.32 = (bf16[1280,384]{1,0:T(8,128)(2,1)S(1)}, bf16[1280,384]{1,0:T(8,128)(2,1)}, u32[]{:S(2)}, u32[]{:S(2)}) collective-permute-start(bf16[1280,384]{1,0:T(8,128)(2,1)S(1)} %constant_dynamic-update-slice_fusion.g00_ref), channel_id=1, source_target_pairs={{0,1},{1,0},{2,3},{3,2},{4,5},{5,4},{6,7},{7,6},{8,9},{9,8},{10,11... | collective-permute-start | bytes 2949128 | tf_op jit(solution)/shard_map/ppermute | solution.py:65
  165.2 6.3 %collective-permute-start.24 = (bf16[216,104]{1,0:T(8,128)(2,1)S(1)}, bf16[216,104]{1,0:T(8,128)(2,1)S(1)}, u32[]{:S(2)}, u32[]{:S(2)}) collective-permute-start(bf16[216,104]{1,0:T(8,128)(2,1)S(1)} %add_convert_fusion.1), channel_id=1, source_target_pairs={{0,16},{1,17},{2,18},{3,19},{4,20},{5,21},{6,22},{7,23},{8,24},{9,... | collective-permute-start | bytes 134792 | tf_op jit(solution)/shard_map/ppermute | solution.py:65
  180.7 42.1 %collective-permute-start.27 = (bf16[864,104]{1,0:T(8,128)(2,1)S(1)}, bf16[864,104]{1,0:T(8,128)(2,1)}, u32[]{:S(2)}, u32[]{:S(2)}) collective-permute-start(bf16[864,104]{1,0:T(8,128)(2,1)S(1)} %maximum_select_fusion.2), channel_id=1, source_target_pairs={{0,1},{1,0},{2,3},{3,2},{4,5},{5,4},{6,7},{7,6},{8,9},{9,8},{10,11... | collective-permute-start | bytes 539144 | tf_op jit(solution)/shard_map/ppermute | solution.py:65
  (19 other events, 214.6 us)

commit v2 on v1

--- a/solution.py
+++ b/solution.py
@@ -25,12 +25,11 @@
     angles = phases * np.float32(2.0 * math.pi / width)
     scaling = np.float32(1.0 / math.sqrt(width))
     table = np.concatenate([np.cos(angles) * scaling, -np.sin(angles) * scaling], axis=1)
+    base = jnp.asarray(table, dtype=bf16)
     span = 2 * modes
     reach = max(round_up(b * span % LANE + span, LANE) for b in range(batch))
-    full = np.zeros((batch, width, reach), np.float32)
-    for b in range(batch):
-        full[b, :, b * span % LANE : b * span % LANE + span] = table
-    return jnp.asarray(full, dtype=bf16)
+    starts = [b * span % LANE for b in range(batch)]
+    return jnp.stack([jnp.pad(base, ((0, 0), (start, reach - start - span))) for start in starts])
 
 
 class Plan:
@@ -48,6 +47,7 @@
             second[1], second[2] = second[2], second[1]
         self.orders = (first, second)
         self.rest = list(range(self.halvings, bits))
+        self.turns = [[turn] for turn in range(self.halvings)]
 
     def flips(self, color):
         order = self.orders[color]
@@ -60,30 +60,70 @@
             masks.append(mask)
         return np.asarray(masks, dtype=np.int32)
 
+    def masks(self, color, turn):
+        bits = [self.orders[color][t] for t in self.turns[turn]]
+        return [
+            sum(1 << bit for place, bit in enumerate(bits) if part >> (len(bits) - 1 - place) & 1)
+            for part in range(1, 1 << len(bits))
+        ]
+
+    def trade(self, value, mask):
+        return lax.ppermute(value, AXES, [(i, i ^ mask) for i in range(self.total)])
+
     def swap(self, value, bit):
-        pairs = [(i, i ^ (1 << bit)) for i in range(self.total)]
-        return lax.ppermute(value, AXES, pairs)
-
-
-def reduce_scatter(plan, color, keep, send):
-    for turn, bit in enumerate(plan.orders[color]):
-        total = keep + plan.swap(send, bit).astype(f32)
-        if turn + 1 < plan.halvings:
-            middle = total.shape[0] // 2
-            keep, send = total[:middle], total[middle:].astype(bf16)
+        return self.trade(value, 1 << bit)
+
+
+def first_exchange(plan, keep, send):
+    if plan.halvings == 0:
+        return keep
+    return keep + plan.swap(send, plan.orders[0][0]).astype(f32)
+
+
+def reduce_scatter(plan, fields, late):
+    keeps = [jnp.stack([field[color] for field in fields]) for color in range(2)]
+    arrived = []
+    for turn in range(1, len(plan.turns)):
+        keeps = [sum([other[color].astype(f32) for other in arrived], keeps[color]) for color in range(2)]
+        if turn == 2:
+            keeps, late = lax.optimization_barrier((keeps, late))
+        parts = 1 << len(plan.turns[turn])
+        size = keeps[0].shape[1] // parts
+        masks = [plan.masks(color, turn) for color in range(2)]
+        arrived = []
+        for part in range(1, parts):
+            sends = [keep[:, part * size : (part + 1) * size].astype(bf16) for keep in keeps]
+            if masks[0] == masks[1]:
+                arrived.append(plan.trade(jnp.stack(sends), masks[0][part - 1]))
+            else:
+                arrived.append([plan.trade(sends[color], masks[color][part - 1]) for color in range(2)])
+        keeps = [keep[:, :size] for keep in keeps]
+    keep = jnp.stack(keeps)
+    arrived = [other if isinstance(other, jax.Array) else jnp.stack(other) for other in arrived]
     for bit in plan.rest:
-        value = total.astype(bf16)
-        total = value.astype(f32) + plan.swap(value, bit).astype(f32)
-    return total
-
-
-def all_gather(plan, color, value):
-    other = value
-    for turn, bit in enumerate(reversed(plan.orders[color])):
-        if turn > 0:
-            value = jnp.concatenate([value, other], axis=0)
-        other = plan.swap(value, bit)
-    return value, other
+        value = sum([other.astype(f32) for other in arrived], keep).astype(bf16)
+        keep, arrived = value.astype(f32), [plan.swap(value, bit)]
+    return keep, arrived, late
+
+
+def all_gather(plan, both):
+    values = None
+    for turn in reversed(range(len(plan.turns))):
+        masks = [plan.masks(color, turn) for color in range(2)]
+        if values is None:
+            if masks[0] == masks[1]:
+                others = [plan.trade(both, mask) for mask in masks[0]]
+            else:
+                others = list(zip(*[[plan.trade(both[color], mask) for mask in masks[color]] for color in range(2)]))
+            values = [both[0], both[1]]
+        else:
+            values = [jnp.concatenate([values[color]] + [o[color] for o in others], axis=0) for color in range(2)]
+            if masks[0] == masks[1] and turn > 0:
+                both = jnp.stack(values)
+                others = [plan.trade(both, mask) for mask in masks[0]]
+                continue
+            others = list(zip(*[[plan.trade(values[color], mask) for mask in masks[color]] for color in range(2)]))
+    return [values[0], others[0][0], values[1], others[0][1]]
 
 
 def column_tables(plan, kept, rows_here, height, me, shard):
@@ -116,12 +156,12 @@
 
 
 def forward_kernel(
-    x_ref, table_ref, factor_ref, forth_ref, rows_ref, keep0_ref, send0_ref, keep1_ref, send1_ref,
+    x_ref, table_ref, factor_ref, forth_ref, rows_ref, keep_ref, send_ref,
     raw, projected, packed, *, plan, rank, rows_here,
 ):
     step = pl.program_id(0)
     batch, channels, block, width = x_ref.shape
-    lanes = keep0_ref.shape[1]
+    lanes = keep_ref.shape[1]
     span = lanes // batch
     modes = span // 2
     tiles = lanes // LANE
@@ -130,23 +170,31 @@
     rank_pad = factor_ref.shape[0]
     segment = packed.shape[1] // (2 * plan.owners)
     reach = table_ref.shape[2] // LANE
+    gap = block + 8
+    some = max(1, 256 // block)
     for b in range(batch):
-        values = jnp.dot(x_ref[b].reshape(channels * block, width), table_ref[b], preferred_element_type=f32)
-        for t in range(reach):
-            raw[b * reach + t] = values[:, t * LANE : (t + 1) * LANE]
+        for first in range(0, channels, some):
+            values = jnp.dot(
+                x_ref[b, first : first + some].reshape(some * block, width), table_ref[b], preferred_element_type=f32
+            )
+            for t in range(reach):
+                for i in range(some):
+                    raw[b * reach + t, (first + i) * gap : (first + i) * gap + block] = values[
+                        i * block : (i + 1) * block, t * LANE : (t + 1) * LANE
+                    ]
     for h in range(block):
         parts = [None] * tiles
         for b in range(batch):
             for t in range(reach):
                 place = b * span // LANE + t
                 if place < tiles:
-                    piece = raw[b * reach + t, pl.ds(h, channels, stride=block), :]
+                    piece = raw[b * reach + t, pl.ds(h, channels, stride=gap), :]
                     parts[place] = piece if parts[place] is None else parts[place] + piece
         joined = jnp.concatenate(parts, axis=1).astype(bf16)
         rows_ref[:, h * lanes : (h + 1) * lanes] = joined
         mixed = jnp.dot(factor_ref[...], joined, preferred_element_type=f32)
         for t in range(tiles):
-            projected[t, pl.ds(step * block + h, rank_pad, stride=rows_here), :] = mixed[:, t * LANE : (t + 1) * LANE]
+            projected[t, pl.ds(step * block + h, rank_pad, stride=rows_here + 8), :] = mixed[:, t * LANE : (t + 1) * LANE]
 
     @pl.when(step == pl.num_programs(0) - 1)
     def _():
@@ -159,9 +207,9 @@
                         )
         for color in range(2):
 
-            @pl.loop(0, half)
+            @pl.loop(0, half, unroll=True)
             def _(a):
-                start = pl.multiple_of((color * half + a) * rows_here, 8)
+                start = pl.multiple_of((color * half + a) * (rows_here + 8), 8)
                 plane = jnp.concatenate(
                     [projected[t, pl.ds(start, rows_here), :] for t in range(tiles)], axis=1
                 ).astype(bf16)
@@ -173,12 +221,12 @@
                             t, pl.ds(color * plan.owners * segment + j * half + a, plan.owners, stride=segment), :
                         ] = spectrum[j * plan.owners : (j + 1) * plan.owners, t * LANE : (t + 1) * LANE]
 
-        middle = keep0_ref.shape[0]
+        middle = keep_ref.shape[0] // 2
         for t in range(tiles):
-            for color, (keep_ref, send_ref) in enumerate(((keep0_ref, send0_ref), (keep1_ref, send1_ref))):
-                start = 2 * color * middle
-                keep_ref[:, t * LANE : (t + 1) * LANE] = packed[t, start : start + middle]
-                send_ref[:, t * LANE : (t + 1) * LANE] = packed[t, start + middle : start + 2 * middle].astype(bf16)
+            for color in range(2):
+                here, start = slice(color * middle, (color + 1) * middle), 2 * color * middle
+                keep_ref[here, t * LANE : (t + 1) * LANE] = packed[t, start : start + middle]
+                send_ref[here, t * LANE : (t + 1) * LANE] = packed[t, start + middle : start + 2 * middle].astype(bf16)
 
 
 def forward(plan, field, table, factor, forth, rank, modes):
@@ -202,14 +250,14 @@
         out_specs=[
             pl.BlockSpec((channels, block * lanes), lambda s: (0, s)),
         ]
-        + [pl.BlockSpec((middle, lanes), lambda s: (0, 0))] * 4,
+        + [pl.BlockSpec((2 * middle, lanes), lambda s: (0, 0))] * 2,
         out_shape=[
             jax.ShapeDtypeStruct((channels, rows_here * lanes), bf16),
         ]
-        + [jax.ShapeDtypeStruct((middle, lanes), dtype) for dtype in (f32, bf16, f32, bf16)],
+        + [jax.ShapeDtypeStruct((2 * middle, lanes), dtype) for dtype in (f32, bf16)],
         scratch_shapes=[
-            pltpu.VMEM((batch * table.shape[2] // LANE, channels * block, LANE), f32),
-            pltpu.VMEM((lanes // LANE, rank_pad * rows_here, LANE), f32),
+            pltpu.VMEM((batch * table.shape[2] // LANE, channels * (block + 8), LANE), f32),
+            pltpu.VMEM((lanes // LANE, rank_pad * (rows_here + 8), LANE), f32),
             pltpu.VMEM((lanes // LANE, 2 * plan.owners * segment, LANE), f32),
         ],
         compiler_params=pltpu.CompilerParams(vmem_limit_bytes=VMEM_LIMIT),
@@ -222,33 +270,37 @@
 
 
 def backward_kernel(
-    g00_ref, g01_ref, g10_ref, g11_ref, rows_in_ref, rows_out_ref, back_ref, out_in_ref, out_out_ref,
+    g00_ref, g01_ref, g10_ref, g11_ref, rows_in_ref, rows_out_ref, back_ref, out_ref,
     wide, grids_in, grids_out, block_in, block_out, *, plan, ranks, rows_here, modes,
 ):
     step = pl.program_id(0)
     tiles = wide.shape[0]
     lanes = tiles * LANE
     segments = [round_up(plan.per * rank // 2, 8) for rank in ranks]
-    stride = sum(segments)
+    used = sum(segments)
+    stride = used + (8 if used // 8 % 2 == 0 else 16)
+    channels = rows_in_ref.shape[0]
 
     @pl.when(step == 0)
     def _():
-        out_in_ref[...] = jnp.zeros_like(out_in_ref)
-        out_out_ref[...] = jnp.zeros_like(out_out_ref)
+        out_ref[...] = jnp.zeros_like(out_ref)
         for grids, rank in zip((grids_in, grids_out), ranks):
-            spare = grids.shape[1] - rank * rows_here
+            spare = grids.shape[1] - rank * (rows_here + 8)
             if spare:
-                grids[:, rank * rows_here :, :] = jnp.zeros((tiles, spare, LANE), f32)
+                grids[:, rank * (rows_here + 8) :, :] = jnp.zeros((tiles, spare, LANE), f32)
         for color, (one, other) in enumerate(((g00_ref, g01_ref), (g10_ref, g11_ref))):
-            middle = one.shape[0]
             for t in range(tiles):
-                wide[t, :middle, :] = one[:, t * LANE : (t + 1) * LANE].astype(f32)
-                wide[t, middle:, :] = other[:, t * LANE : (t + 1) * LANE].astype(f32)
+                for relative in range(plan.owners):
+                    piece = one if relative < plan.owners // 2 else other
+                    start = relative % (plan.owners // 2) * used
+                    wide[t, relative * stride : relative * stride + used, :] = piece[
+                        start : start + used, t * LANE : (t + 1) * LANE
+                    ].astype(f32)
             for side, (grids, rank) in enumerate(zip((grids_in, grids_out), ranks)):
                 half = rank // 2
                 base = side * segments[0]
 
-                @pl.loop(0, half)
+                @pl.loop(0, half, unroll=True)
                 def _(a):
                     spectrum = jnp.concatenate(
                         [
@@ -264,21 +316,20 @@
                         axis=0,
                     ).astype(bf16)
                     both = jnp.dot(back_ref[color], spectrum, preferred_element_type=f32)
-                    start = pl.multiple_of((color * half + a) * rows_here, 8)
+                    start = pl.multiple_of((color * half + a) * (rows_here + 8), 8)
                     grid = both[:rows_here] + turned(both[rows_here:], modes, -1)
                     for t in range(tiles):
                         grids[t, pl.ds(start, rows_here), :] = grid[:, t * LANE : (t + 1) * LANE]
 
-    for grids, block_ref, rows_ref, out_ref in (
-        (grids_in, block_in, rows_in_ref, out_in_ref),
-        (grids_out, block_out, rows_out_ref, out_out_ref),
+    for side, (grids, block_ref, rows_ref) in enumerate(
+        ((grids_in, block_in, rows_in_ref), (grids_out, block_out, rows_out_ref))
     ):
         for h in range(block_ref.shape[1] // lanes):
             for t in range(tiles):
                 block_ref[:, h * lanes + t * LANE : h * lanes + (t + 1) * LANE] = grids[
-                    t, pl.ds(step * (block_ref.shape[1] // lanes) + h, block_ref.shape[0], stride=rows_here), :
+                    t, pl.ds(step * (block_ref.shape[1] // lanes) + h, block_ref.shape[0], stride=rows_here + 8), :
                 ].astype(bf16)
-        out_ref[...] += lax.dot_general(
+        out_ref[side * channels : (side + 1) * channels, : block_ref.shape[0]] += lax.dot_general(
             rows_ref[...], block_ref[...], (((1,), (1,)), ((), ())), preferred_element_type=f32
         )
 
@@ -295,10 +346,10 @@
         grid=(rows_here // block,),
         in_specs=[pl.BlockSpec(piece.shape, whole) for piece in pieces]
         + [part, part, pl.BlockSpec(back.shape, lambda s: (0, 0, 0))],
-        out_specs=[pl.BlockSpec((channels, pad), whole) for pad in pads],
-        out_shape=[jax.ShapeDtypeStruct((channels, pad), f32) for pad in pads],
-        scratch_shapes=[pltpu.VMEM((lanes // LANE, 2 * pieces[0].shape[0], LANE), f32)]
-        + [pltpu.VMEM((lanes // LANE, pad * rows_here, LANE), f32) for pad in pads]
+        out_specs=pl.BlockSpec((2 * channels, max(pads)), whole),
+        out_shape=jax.ShapeDtypeStruct((2 * channels, max(pads)), f32),
+        scratch_shapes=[pltpu.VMEM((lanes // LANE, 2 * pieces[0].shape[0] + 16 * plan.owners, LANE), f32)]
+        + [pltpu.VMEM((lanes // LANE, pad * (rows_here + 8), LANE), f32) for pad in pads]
         + [pltpu.VMEM((pad, block * lanes), bf16) for pad in pads],
         compiler_params=pltpu.CompilerParams(vmem_limit_bytes=VMEM_LIMIT),
         cost_estimate=pl.CostEstimate(
@@ -310,19 +361,19 @@
 
 
 def owner_kernel(
-    left0_ref, left1_ref, right0_ref, right1_ref, core_ref, core_t_ref, modes_ref, height_ref, width_ref,
-    core_out, height_out, width_out, back0_ref, back1_ref, modal, pair, pair_low,
-    *, plan, batch, rank_in, rank_out, modes,
+    keep_ref, core_ref, core_t_ref, modes_ref, height_ref, width_ref, *refs, plan, batch, rank_in, rank_out, modes,
 ):
     pad_in, pad_out = round_up(rank_in, 8), round_up(rank_out, 8)
-    lanes = left0_ref.shape[1]
+    lanes = keep_ref.shape[3]
     plane = modes_ref.shape[2]
-    segment_in = left0_ref.shape[0]
+    segment_in = keep_ref.shape[2]
+    *arrived, core_out, height_out, width_out, back_ref, modal, pair, pair_low, returned = refs
+    sums = [sum([ref[:, side].astype(f32) for ref in arrived], keep_ref[:, side]) for side in range(2)]
     rows = rank_in * pad_out
 
-    def gathered(refs, j, rank, pad):
+    def gathered(sums, j, rank, pad):
         half = rank // 2
-        parts = [ref[...].astype(f32)[j * half : (j + 1) * half] for ref in refs]
+        parts = [sums[color, j * half : (j + 1) * half] for color in range(2)]
         if pad > rank:
             parts.append(jnp.zeros((pad - rank, lanes), f32))
         joined = jnp.concatenate(parts, axis=0)
@@ -347,8 +398,8 @@
     core_sum = None
     width_sum = None
     for j in range(plan.per):
-        left = gathered((left0_ref, left1_ref), j, rank_in, pad_in)
-        right = gathered((right0_ref, right1_ref), j, rank_out, pad_out)
+        left = gathered(sums[0], j, rank_in, pad_in)
+        right = gathered(sums[1], j, rank_out, pad_out)
         table = modes_ref[j].astype(bf16)
         table_low = (modes_ref[j] - table.astype(f32)).astype(bf16)
         modal[...] = (
@@ -401,29 +452,30 @@
         half_in, half_out = rank_in // 2, rank_out // 2
         inward_all = spread([jnp.concatenate(rows_of, axis=0) for rows_of in inward])
         outward_all = spread(outward)
-        for color, ref in enumerate((back0_ref, back1_ref)):
-            ref[j * half_in : (j + 1) * half_in] = inward_all[color * half_in : (color + 1) * half_in]
-            ref[segment_in + j * half_out : segment_in + (j + 1) * half_out] = outward_all[
+        for color in range(2):
+            returned[color, j * half_in : (j + 1) * half_in] = inward_all[color * half_in : (color + 1) * half_in]
+            returned[color, segment_in + j * half_out : segment_in + (j + 1) * half_out] = outward_all[
                 color * half_out : (color + 1) * half_out
             ]
-    for ref in (back0_ref, back1_ref):
+    for color in range(2):
         for start, used, stop in (
             (0, plan.per * rank_in // 2, segment_in),
-            (segment_in, plan.per * rank_out // 2, ref.shape[0]),
+            (segment_in, plan.per * rank_out // 2, returned.shape[1]),
         ):
             if start + used < stop:
-                ref[start + used : stop] = jnp.zeros((stop - start - used, lanes), f32)
+                returned[color, start + used : stop] = jnp.zeros((stop - start - used, lanes), f32)
+    back_ref[...] = returned[...].astype(bf16)
     width_out[...] = width_sum
 
 
-def owner_work(plan, left, right, core_tensor, height_rows, width_factor, batch):
+def owner_work(plan, keep, arrived, core_tensor, height_rows, width_factor, batch):
     _, rank_in, rank_out, rank_x, rank_y = core_tensor.shape
     modes = width_factor.shape[0]
     pad_out = round_up(rank_out, 8)
     pairs = round_up(rank_x * rank_y, 8)
     plane = round_up(modes, 128)
-    lanes = left[0].shape[1]
-    rows = left[0].shape[0] + right[0].shape[0]
+    lanes = keep.shape[3]
+    rows = 2 * keep.shape[2]
     spare = pairs - rank_x * rank_y
     core = core_tensor.reshape(2, rank_in, rank_out, rank_x * rank_y)
     core = jnp.pad(core, ((0, 0), (0, 0), (0, pad_out - rank_out), (0, spare)))
@@ -436,7 +488,7 @@
     height_wide = jnp.broadcast_to(height_rows[:, :, None], (plan.per, rank_x, rank_y))
     height_wide = jnp.pad(height_wide.reshape(plan.per, rank_x * rank_y, 1), ((0, 0), (0, spare), (0, 0)))
     table = height_wide * width_wide[None]
-    core_part, height_part, width_part, back0, back1 = pl.pallas_call(
+    core_part, height_part, width_part, back = pl.pallas_call(
         functools.partial(
             owner_kernel, plan=plan, batch=batch, rank_in=rank_in, rank_out=rank_out, modes=modes
         ),
@@ -444,40 +496,49 @@
             jax.ShapeDtypeStruct((2 * rank_in * pad_out, pairs), f32),
             jax.ShapeDtypeStruct((plan.per, pairs, 1), f32),
             jax.ShapeDtypeStruct((pairs, plane), f32),
-            jax.ShapeDtypeStruct((rows, lanes), f32),
-            jax.ShapeDtypeStruct((rows, lanes), f32),
+            jax.ShapeDtypeStruct((2, rows, lanes), bf16),
         ],
         scratch_shapes=[
             pltpu.VMEM((2 * rank_in * pad_out, plane), f32),
             pltpu.VMEM((2 * rank_in * pad_out, plane), bf16),
             pltpu.VMEM((2 * rank_in * pad_out, plane), bf16),
+            pltpu.VMEM((2, rows, lanes), f32),
         ],
         compiler_params=pltpu.CompilerParams(vmem_limit_bytes=VMEM_LIMIT),
-    )(*left, *right, core, jnp.swapaxes(core, 1, 2), table, height_wide, width_wide)
+    )(keep, core, jnp.swapaxes(core, 1, 2), table, height_wide, width_wide, *arrived)
     height_part = height_part[:, : rank_x * rank_y, 0].reshape(plan.per, rank_x, rank_y).sum(axis=2)
     width_part = width_part[: rank_x * rank_y, :modes].reshape(rank_x, rank_y, modes).sum(axis=0)
-    return core_part, height_part, width_part, (back0.astype(bf16), back1.astype(bf16))
+    return core_part, height_part, width_part, back
+
+
+def exchange_sum(plan, bits, value):
+    terms = [value.astype(f32)]
+    for part in range(1, 1 << len(bits)):
+        mask = sum(1 << bit for place, bit in enumerate(bits) if part >> place & 1)
+        terms.append(plan.trade(value, mask).astype(f32))
+    while len(terms) > 1:
+        terms = [one + other for one, other in zip(terms[::2], terms[1::2])]
+    return terms[0]
 
 
 def all_reduce(plan, bits, value):
     for bit in bits:
-        value = value + plan.swap(value, bit)
+        value = exchange_sum(plan, [bit], value)
     return value
 
 
 def all_reduce_large(plan, me, value):
     split = []
-    for bit in range(plan.total.bit_length() - 1):
-        if value.shape[0] % 16 == 0 and len(split) < 3:
-            middle = value.shape[0] // 2
-            high = (me >> bit) & 1
-            keep = lax.dynamic_slice_in_dim(value, high * middle, middle, 0)
-            send = lax.dynamic_slice_in_dim(value, (1 - high) * middle, middle, 0).astype(bf16)
-            value = keep + plan.swap(send, bit).astype(f32)
-            split.append((bit, high))
-        else:
-            sent = value.astype(bf16)
-            value = sent.astype(f32) + plan.swap(sent, bit).astype(f32)
+    bits = list(range(plan.total.bit_length() - 1))
+    for bit in bits[:3]:
+        middle = value.shape[0] // 2
+        high = (me >> bit) & 1
+        keep = lax.dynamic_slice_in_dim(value, high * middle, middle, 0)
+        send = lax.dynamic_slice_in_dim(value, (1 - high) * middle, middle, 0).astype(bf16)
+        value = keep + plan.swap(send, bit).astype(f32)
+        split.append((bit, high))
+    for bit in bits[3:]:
+        value = exchange_sum(plan, [bit], value.astype(bf16))
     value = value.astype(bf16)
     for bit, high in reversed(split):
         other = plan.swap(value, bit)
@@ -503,22 +564,24 @@
         rank = factor.shape[1]
         return jnp.pad(factor.T, ((0, round_up(rank, 8) - rank), (0, 0)))
 
-    def scattered(parts):
-        return [reduce_scatter(plan, color, parts[2 * color], parts[2 * color + 1]) for color in range(2)]
+    def exchanged(parts):
+        total = first_exchange(plan, *parts)
+        return total.reshape(2, total.shape[0] // 2, total.shape[1])
 
     rows_input, *left = forward(plan, inputs, table, padded(input_factor), forth, rank_in, modes)
-    left = scattered(left)
+    left = exchanged(left)
     rows_cot, *right = forward(plan, cotangent, table, padded(output_factor), forth, rank_out, modes)
-    right = scattered(right)
+    right = exchanged(right)
+    keep, arrived, (core_tensor, height_factor, width_factor) = reduce_scatter(
+        plan, (left, right), (core_tensor, height_factor, width_factor)
+    )
 
     owner = me & (plan.owners - 1)
     height_rows = height_factor[jnp.arange(plan.per) * plan.owners + owner]
     core_part, height_part, width_part, back_parts = owner_work(
-        plan, left, right, core_tensor, height_rows, width_factor, batch
+        plan, keep, arrived, core_tensor, height_rows, width_factor, batch
     )
-    pieces = []
-    for color in range(2):
-        pieces.extend(all_gather(plan, color, back_parts[color]))
+    pieces = all_gather(plan, back_parts)
 
     counts = (me >> plan.halvings) == 0
     height_full = jnp.zeros((plan.per, plan.owners, rank_x), f32)
@@ -540,13 +603,9 @@
     height_grad = summed[core_rows : core_rows + rank_x, :kept].T
     width_grad = summed[core_rows + rank_x : core_rows + rank_x + rank_y, :modes].T
 
-    input_part, output_part = backward(
-        plan, pieces, rows_input, rows_cot, back, (rank_in, rank_out), rows_here, modes
-    )
-    input_part, output_part = input_part[:, :rank_in], output_part[:, :rank_out]
-    over_rows = range(blocks.bit_length() - 1, plan.total.bit_length() - 1)
-    both = all_reduce(plan, over_rows, jnp.concatenate([input_part, output_part], axis=0))
-    return (core_grad, both[:channels], both[channels:], height_grad, width_grad)
+    both = backward(plan, pieces, rows_input, rows_cot, back, (rank_in, rank_out), rows_here, modes)
+    both = all_reduce(plan, range(blocks.bit_length() - 1, plan.total.bit_length() - 1), both)
+    return (core_grad, both[:channels, :rank_in], both[channels:, :rank_out], height_grad, width_grad)
 
 
 def solution(mesh):

time: 232 us -> 193 us (0.83)
  Pallas kernels: 109 us -> 73.7 us
  starting transfers between devices: 42.6 us -> 31.5 us
  waiting for transfers between devices: 44.2 us -> 53.5 us
  other arithmetic: 16.5 us -> 12.6 us
    pallas_call x2, Pallas kernels: 66.8 us -> 48.7 us  [forward(): pl.pallas_call(functools.partial(forward_kernel, plan=plan, rank=rank, ro...]
    pallas_call x1, Pallas kernels: 34.6 us -> 17.6 us  [backward(): pl.pallas_call(functools.partial(backward_kernel, plan=plan, ranks=ranks,...]
    ppermute x41 -> x27, starting transfers between devices: 42.6 us -> 31.5 us  [trade(): return lax.ppermute(value, AXES, [(i, i ^ mask) for i in range(self.total)])]
    ppermute x41 -> x27, waiting for transfers between devices: 44.2 us -> 53.5 us  [trade(): return lax.ppermute(value, AXES, [(i, i ^ mask) for i in range(self.total)])]
    add x23 -> x10, other arithmetic: 6.64 us -> 3.99 us  [the longest x5 2.8 us: reduce_scatter(): sum([other[color].astype(f32) for other in arrived], keeps[color])]
    unnamed x27 -> x39, local copies, waits for them, and re-layouts: 1.22 us -> 3.79 us
  transfers between devices with their start and end apart: 41 -> 27, of which waited for: 19 -> 18; matrix products, arithmetic and copies ran while one was open for 12% -> 12% of each run, Pallas kernels for 29% -> 22%
where the time goes in v2:
time: 193 us; the launch traced here: 192 us
  Pallas kernels  73.7 us (38%)
  waiting for transfers between devices  53.5 us (28%)
  starting transfers between devices  31.5 us (16%)
  local copies, waits for them, and re-layouts  19.8 us (10%)
  other arithmetic  12.6 us (7%)
    ppermute x27, waiting for transfers between devices, trade(): return lax.ppermute(value, AXES, [(i, i ^ mask) for i in range(self.total)])  53.5 us
    pallas_call x2, Pallas kernels, forward(): pl.pallas_call(functools.partial(forward_kernel, plan=plan, rank=rank, ro...  48.7 us
    ppermute x27, starting transfers between devices, trade(): return lax.ppermute(value, AXES, [(i, i ^ mask) for i in range(self.total)])  31.5 us
    pallas_call x1, Pallas kernels, backward(): pl.pallas_call(functools.partial(backward_kernel, plan=plan, ranks=ranks,...  17.6 us
    pallas_call x1, Pallas kernels, owner_work(): pl.pallas_call(functools.partial(owner_kernel, plan=plan, batch=batch, ra...  7.4 us
  transfers between devices with their start and end apart: 27, of which 18 were waited for; matrix products, arithmetic and copies ran while one was open for 12% of the time, Pallas kernels for 22%

profile of v2, /device:TPU:0, one launch (start us, length us, event | category | flops | bytes accessed | tf_op | source)
XLA Modules:
  0.0 192.4 jit_solution(13303193730524170762)
XLA Ops:
  2.7 1.3 pad.38.factor_ref
  4.0 24.3 %shard_map.129 = (bf16[64,49152]{1,0:T(8,128)(2,1)}, f32[1280,384]{1,0:T(8,128)}, bf16[1280,384]{1,0:T(8,128)(2,1)}) custom-call(bf16[2,64,128,1024]{3,2,1,0:T(8,128)(2,1)} %x_ref.3, bf16[2,1024,256]{2,1,0:T(8,128)(2,1)} %constant.96.table_ref, bf16[32,64]{1,0:T(8,128)(2,1)} %pad.38.factor_ref, bf16[2,192,128]{2,1,0:T(8,128)(2,1)} %pad_maximum_fusion.12.forth_ref), custom_call_target="tpu_custom_call" | custom-call | flops 6442450944 | bytes 39845888 | tf_op jit(solution)/shard_map/pallas_call | solution.py:241
  29.4 24.5 %shard_map.128 = (bf16[64,49152]{1,0:T(8,128)(2,1)}, f32[1280,384]{1,0:T(8,128)}, bf16[1280,384]{1,0:T(8,128)(2,1)}) custom-call(bf16[2,64,128,1024]{3,2,1,0:T(8,128)(2,1)} %x_ref.2, bf16[2,1024,256]{2,1,0:T(8,128)(2,1)} %constant.96.table_ref, bf16[32,64]{1,0:T(8,128)(2,1)} %pad.37.factor_ref, bf16[2,192,128]{2,1,0:T(8,128)(2,1)} %pad_maximum_fusion.12.forth_ref), custom_call_target="tpu_custom_call" | custom-call | flops 6442450944 | bytes 39845888 | tf_op jit(solution)/shard_map/pallas_call | solution.py:241
  54.2 2.4 %collective-permute-done = bf16[1280,384]{1,0:T(8,128)(2,1)S(1)} collective-permute-done((bf16[1280,384]{1,0:T(8,128)(2,1)}, bf16[1280,384]{1,0:T(8,128)(2,1)S(1)}, u32[]{:S(2)}, u32[]{:S(2)}) %collective-permute-start) | collective-permute-done | bytes 983072 | tf_op jit(solution)/shard_map/ppermute | solution.py:71
  57.9 2.6 %collective-permute-start.3 = (bf16[2,320,384]{2,1,0:T(8,128)(2,1)}, bf16[2,320,384]{2,1,0:T(8,128)(2,1)}, u32[]{:S(2)}, u32[]{:S(2)}) collective-permute-start(bf16[2,320,384]{2,1,0:T(8,128)(2,1)} %fusion.4), channel_id=1, source_target_pairs={{0,4},{1,5},{2,6},{3,7},{4,0},{5,1},{6,2},{7,3},{8,12},{9,13},{10,... | collective-permute-start | bytes 1474568 | tf_op jit(solution)/shard_map/ppermute | solution.py:71
  60.6 1.6 collective-permute-start.2
  62.2 10.4 %collective-permute-done.3 = bf16[2,320,384]{2,1,0:T(8,128)(2,1)} collective-permute-done((bf16[2,320,384]{2,1,0:T(8,128)(2,1)}, bf16[2,320,384]{2,1,0:T(8,128)(2,1)}, u32[]{:S(2)}, u32[]{:S(2)}) %collective-permute-start.3) | collective-permute-done | bytes 491552 | tf_op jit(solution)/shard_map/ppermute | solution.py:71
  74.0 1.4 fusion.3
  75.4 1.8 collective-permute-start.5
  77.3 1.6 collective-permute-start.4
  79.7 3.4 %copy.21 = f32[2,26,26,100]{3,2,1,0:T(8,128)S(1)} copy(f32[2,26,26,100]{2,0,3,1:T(2,128)} %bitcast.81) | data formatting | bytes 1081600 | tf_op jit(solution)/shard_map/reshape | solution.py:480
  85.5 1.6 collective-permute-start.6
  89.9 2.5 %collective-permute-done.6 = bf16[2,2,80,384]{3,2,1,0:T(8,128)(2,1)S(1)} collective-permute-done((bf16[2,2,80,384]{3,2,1,0:T(8,128)(2,1)S(1)}, bf16[2,2,80,384]{3,2,1,0:T(8,128)(2,1)S(1)}, u32[]{:S(2)}, u32[]{:S(2)}) %collective-permute-start.6) | collective-permute-done | bytes 245792 | tf_op jit(solution)/shard_map/ppermute | solution.py:71
  92.4 2.7 %collective-permute-start.7 = (bf16[2,2,40,384]{3,2,1,0:T(8,128)(2,1)S(1)}, bf16[2,2,40,384]{3,2,1,0:T(8,128)(2,1)S(1)}, u32[]{:S(2)}, u32[]{:S(2)}) collective-permute-start(bf16[2,2,40,384]{3,2,1,0:T(8,128)(2,1)S(1)} %pad_maximum_fusion.11), channel_id=1, source_target_pairs={{0,16},{1,17},{2,18},{3,19},{4,20},{5,21},{6,22},{7,23},{8,24},{9,... | collective-permute-start | bytes 368648 | tf_op jit(solution)/shard_map/ppermute | solution.py:71
  95.8 3.8 %collective-permute-done.7.refs_0_ = bf16[2,2,40,384]{3,2,1,0:T(8,128)(2,1)S(1)} collective-permute-done((bf16[2,2,40,384]{3,2,1,0:T(8,128)(2,1)S(1)}, bf16[2,2,40,384]{3,2,1,0:T(8,128)(2,1)S(1)}, u32[]{:S(2)}, u32[]{:S(2)}) %collective-permute-start.7) | collective-permute-done | bytes 122912 | tf_op jit(solution)/shard_map/ppermute | solution.py:71
  100.3 7.4 %shard_map.130 = (f32[1664,104]{1,0:T(8,128)}, f32[3,104,1]{2,1,0:T(8,128)}, f32[104,128]{1,0:T(8,128)}, bf16[2,80,384]{2,1,0:T(8,128)(2,1)}) custom-call(f32[2,2,40,384]{3,2,1,0:T(8,128)} %pad_maximum_fusion.6.keep_ref, bf16[2,1664,104]{2,1,0:T(8,128)(2,1)} %copy.26.core_ref, bf16[2,104,1664]{2,1,0:T(8,128)(2,1)} %get-tuple-element.51.core_t_ref, ...), custom_call_target="tpu_custom_call" | custom-call | tf_op jit(solution)/shard_map/pallas_call | solution.py:491
  107.7 1.4 collective-permute-start.16
  115.2 1.3 collective-permute-start.9
  116.5 2.7 %collective-permute-start.17 = (bf16[2,160,384]{2,1,0:T(8,128)(2,1)S(1)}, bf16[2,160,384]{2,1,0:T(8,128)(2,1)S(1)}, u32[]{:S(2)}, u32[]{:S(2)}) collective-permute-start(bf16[2,160,384]{2,1,0:T(8,128)(2,1)S(1)} %pad_maximum_fusion.7), channel_id=1, source_target_pairs={{0,8},{1,9},{2,10},{3,11},{4,12},{5,13},{6,14},{7,15},{8,0},{9,1},... | collective-permute-start | bytes 737288 | tf_op jit(solution)/shard_map/ppermute | solution.py:71
  121.7 2.9 %collective-permute-done.10 = bf16[216,104]{1,0:T(8,128)(2,1)S(1)} collective-permute-done((bf16[216,104]{1,0:T(8,128)(2,1)S(1)}, bf16[216,104]{1,0:T(8,128)(2,1)S(1)}, u32[]{:S(2)}, u32[]{:S(2)}) %collective-permute-start.10) | collective-permute-done | bytes 44960 | tf_op jit(solution)/shard_map/ppermute | solution.py:71
  124.7 3.4 %collective-permute-start.11 = (bf16[216,104]{1,0:T(8,128)(2,1)S(1)}, bf16[216,104]{1,0:T(8,128)(2,1)S(1)}, u32[]{:S(2)}, u32[]{:S(2)}) collective-permute-start(bf16[216,104]{1,0:T(8,128)(2,1)S(1)} %add_convert_fusion.2), channel_id=1, source_target_pairs={{0,8},{1,9},{2,10},{3,11},{4,12},{5,13},{6,14},{7,15},{8,0},{9,1},... | collective-permute-start | bytes 134792 | tf_op jit(solution)/shard_map/ppermute | solution.py:71
  131.2 3.2 %collective-permute-done.21 = bf16[320,384]{1,0:T(8,128)(2,1)S(1)} collective-permute-done((bf16[320,384]{1,0:T(8,128)(2,1)S(1)}, bf16[320,384]{1,0:T(8,128)(2,1)S(1)}, u32[]{:S(2)}, u32[]{:S(2)}) %collective-permute-start.21) | collective-permute-done | bytes 245792 | tf_op jit(solution)/shard_map/ppermute | solution.py:71
  136.0 2.5 %collective-permute-start.19 = (bf16[640,384]{1,0:T(8,128)(2,1)S(1)}, bf16[640,384]{1,0:T(8,128)(2,1)S(1)}, u32[]{:S(2)}, u32[]{:S(2)}) collective-permute-start(bf16[640,384]{1,0:T(8,128)(2,1)S(1)} %pad_maximum_fusion.3), channel_id=1, source_target_pairs={{0,2},{1,3},{2,0},{3,1},{4,6},{5,7},{6,4},{7,5},{8,10},{9,11},{10,... | collective-permute-start | bytes 1474568 | tf_op jit(solution)/shard_map/ppermute | solution.py:71
  138.7 6.9 %collective-permute-done.22 = bf16[640,384]{1,0:T(8,128)(2,1)S(1)} collective-permute-done((bf16[640,384]{1,0:T(8,128)(2,1)S(1)}, bf16[640,384]{1,0:T(8,128)(2,1)S(1)}, u32[]{:S(2)}, u32[]{:S(2)}) %collective-permute-start.22) | collective-permute-done | bytes 491552 | tf_op jit(solution)/shard_map/ppermute | solution.py:71
  147.0 3.6 %collective-permute-done.13 = bf16[216,104]{1,0:T(8,128)(2,1)S(1)} collective-permute-done((bf16[216,104]{1,0:T(8,128)(2,1)S(1)}, bf16[216,104]{1,0:T(8,128)(2,1)S(1)}, u32[]{:S(2)}, u32[]{:S(2)}) %collective-permute-start.13) | collective-permute-done | bytes 44960 | tf_op jit(solution)/shard_map/ppermute | solution.py:71
  150.7 1.6 collective-permute-start.14
  152.3 3.3 %collective-permute-done.14 = bf16[432,104]{1,0:T(8,128)(2,1)S(1)} collective-permute-done((bf16[432,104]{1,0:T(8,128)(2,1)S(1)}, bf16[432,104]{1,0:T(8,128)(2,1)S(1)}, u32[]{:S(2)}, u32[]{:S(2)}) %collective-permute-start.14) | collective-permute-done | bytes 89888 | tf_op jit(solution)/shard_map/ppermute | solution.py:71
  157.9 17.6 %shard_map.131 = f32[128,32]{1,0:T(8,128)} custom-call(bf16[1280,384]{1,0:T(8,128)(2,1)} %copy-done.8, bf16[1280,384]{1,0:T(8,128)(2,1)} %collective-permute-done.20.g01_ref, bf16[1280,384]{1,0:T(8,128)(2,1)} %copy-done.7, bf16[1280,384]{1,0:T(8,128)(2,1)} %copy-done.9, bf16[64,49152]{1,0:T(8,128)(2,1)} %get-tuple-element.33.rows_in_ref, ...), custom_call_target="tpu_custom_call" | custom-call | flops 402653184 | bytes 12582912 | tf_op jit(solution)/shard_map/pallas_call | solution.py:344
  176.0 4.2 %collective-permute-done.24 = f32[128,32]{1,0:T(8,128)S(1)} collective-permute-done((f32[128,32]{1,0:T(8,128)}, f32[128,32]{1,0:T(8,128)S(1)}, u32[]{:S(2)}, u32[]{:S(2)}) %collective-permute-start.24) | collective-permute-done | bytes 16416 | tf_op jit(solution)/shard_map/ppermute | solution.py:71
  181.5 3.9 %collective-permute-done.25 = f32[128,32]{1,0:T(8,128)S(1)} collective-permute-done((f32[128,32]{1,0:T(8,128)S(1)}, f32[128,32]{1,0:T(8,128)S(1)}, u32[]{:S(2)}, u32[]{:S(2)}) %collective-permute-start.25) | collective-permute-done | bytes 16416 | tf_op jit(solution)/shard_map/ppermute | solution.py:71
  186.2 2.8 %copy.28 = f32[2,26,26,100]{2,0,3,1:T(2,128)} copy(f32[2,26,26,100]{3,2,1,0:T(8,128)S(1)} %bitcast.80) | data formatting | bytes 1081600 | tf_op jit(solution)/shard_map/slice | solution.py:601
  189.0 2.0 %collective-permute-done.26 = f32[128,32]{1,0:T(8,128)S(1)} collective-permute-done((f32[128,32]{1,0:T(8,128)S(1)}, f32[128,32]{1,0:T(8,128)S(1)}, u32[]{:S(2)}, u32[]{:S(2)}) %collective-permute-start.26) | collective-permute-done | bytes 16416 | tf_op jit(solution)/shard_map/ppermute | solution.py:71
  (158 shorter events, 34.6 us)
Async XLA Ops:
  4.0 24.8 %copy-start.14 = (bf16[64,26]{0,1:T(8,128)(2,1)S(1)}, bf16[64,26]{0,1:T(8,128)(2,1)}, u32[]{:S(2)}) copy-start(bf16[64,26]{0,1:T(8,128)(2,1)} %param.11) | copy-start | bytes 9988
  28.3 25.6 %collective-permute-start.1 = (bf16[1280,384]{1,0:T(8,128)(2,1)}, bf16[1280,384]{1,0:T(8,128)(2,1)S(1)}, u32[]{:S(2)}, u32[]{:S(2)}) collective-permute-start(bf16[1280,384]{1,0:T(8,128)(2,1)} %get-tuple-element.23), channel_id=1, source_target_pairs={{0,1},{1,0},{2,3},{3,2},{4,5},{5,4},{6,7},{7,6},{8,9},{9,8},{10,11... | collective-permute-start | bytes 2949128 | tf_op jit(solution)/shard_map/ppermute | solution.py:71
  29.4 24.5 %copy-start.5 = (f32[1280,384]{1,0:T(8,128)S(1)}, f32[1280,384]{1,0:T(8,128)}, u32[]{:S(2)}) copy-start(f32[1280,384]{1,0:T(8,128)} %get-tuple-element.22) | copy-start | bytes 5898244
  53.9 2.8 %collective-permute-start = (bf16[1280,384]{1,0:T(8,128)(2,1)}, bf16[1280,384]{1,0:T(8,128)(2,1)S(1)}, u32[]{:S(2)}, u32[]{:S(2)}) collective-permute-start(bf16[1280,384]{1,0:T(8,128)(2,1)} %get-tuple-element.21), channel_id=1, source_target_pairs={{0,1},{1,0},{2,3},{3,2},{4,5},{5,4},{6,7},{7,6},{8,9},{9,8},{10,11... | collective-permute-start | bytes 2949128 | tf_op jit(solution)/shard_map/ppermute | solution.py:71
  57.9 14.7 %collective-permute-start.3 = (bf16[2,320,384]{2,1,0:T(8,128)(2,1)}, bf16[2,320,384]{2,1,0:T(8,128)(2,1)}, u32[]{:S(2)}, u32[]{:S(2)}) collective-permute-start(bf16[2,320,384]{2,1,0:T(8,128)(2,1)} %fusion.4), channel_id=1, source_target_pairs={{0,4},{1,5},{2,6},{3,7},{4,0},{5,1},{6,2},{7,3},{8,12},{9,13},{10,... | collective-permute-start | bytes 1474568 | tf_op jit(solution)/shard_map/ppermute | solution.py:71
  60.6 13.4 %collective-permute-start.2 = (bf16[2,320,384]{2,1,0:T(8,128)(2,1)S(1)}, bf16[2,320,384]{2,1,0:T(8,128)(2,1)}, u32[]{:S(2)}, u32[]{:S(2)}) collective-permute-start(bf16[2,320,384]{2,1,0:T(8,128)(2,1)S(1)} %fusion.5), channel_id=1, source_target_pairs={{0,2},{1,3},{2,0},{3,1},{4,6},{5,7},{6,4},{7,5},{8,10},{9,11},{10,... | collective-permute-start | bytes 1474568 | tf_op jit(solution)/shard_map/ppermute | solution.py:71
  75.4 9.2 %collective-permute-start.5 = (bf16[2,160,384]{2,1,0:T(8,128)(2,1)S(1)}, bf16[2,160,384]{2,1,0:T(8,128)(2,1)S(1)}, u32[]{:S(2)}, u32[]{:S(2)}) collective-permute-start(bf16[2,160,384]{2,1,0:T(8,128)(2,1)S(1)} %slice.267), channel_id=1, source_target_pairs={{0,2},{1,3},{2,0},{3,1},{4,6},{5,7},{6,4},{7,5},{8,10},{9,11},{10,... | collective-permute-start | bytes 737288 | tf_op jit(solution)/shard_map/ppermute | solution.py:71
  77.3 7.8 %collective-permute-start.4 = (bf16[2,160,384]{2,1,0:T(8,128)(2,1)S(1)}, bf16[2,160,384]{2,1,0:T(8,128)(2,1)S(1)}, u32[]{:S(2)}, u32[]{:S(2)}) collective-permute-start(bf16[2,160,384]{2,1,0:T(8,128)(2,1)S(1)} %slice.268), channel_id=1, source_target_pairs={{0,4},{1,5},{2,6},{3,7},{4,0},{5,1},{6,2},{7,3},{8,12},{9,13},{10,... | collective-permute-start | bytes 737288 | tf_op jit(solution)/shard_map/ppermute | solution.py:71
  85.5 6.9 %collective-permute-start.6 = (bf16[2,2,80,384]{3,2,1,0:T(8,128)(2,1)S(1)}, bf16[2,2,80,384]{3,2,1,0:T(8,128)(2,1)S(1)}, u32[]{:S(2)}, u32[]{:S(2)}) collective-permute-start(bf16[2,2,80,384]{3,2,1,0:T(8,128)(2,1)S(1)} %pad_maximum_fusion.5), channel_id=1, source_target_pairs={{0,8},{1,9},{2,10},{3,11},{4,12},{5,13},{6,14},{7,15},{8,0},{9,1},... | collective-permute-start | bytes 737288 | tf_op jit(solution)/shard_map/ppermute | solution.py:71
  87.8 7.3 %copy-start.11 = (f32[104,128]{1,0:T(8,128)}, f32[104,128]{1,0:T(8,128)S(1)}, u32[]{:S(2)}) copy-start(f32[104,128]{1,0:T(8,128)S(1)} %pad.42.width_ref) | copy-start | bytes 159748
  92.4 7.2 %collective-permute-start.7 = (bf16[2,2,40,384]{3,2,1,0:T(8,128)(2,1)S(1)}, bf16[2,2,40,384]{3,2,1,0:T(8,128)(2,1)S(1)}, u32[]{:S(2)}, u32[]{:S(2)}) collective-permute-start(bf16[2,2,40,384]{3,2,1,0:T(8,128)(2,1)S(1)} %pad_maximum_fusion.11), channel_id=1, source_target_pairs={{0,16},{1,17},{2,18},{3,19},{4,20},{5,21},{6,22},{7,23},{8,24},{9,... | collective-permute-start | bytes 368648 | tf_op jit(solution)/shard_map/ppermute | solution.py:71
  107.7 7.3 %collective-permute-start.16 = (bf16[2,80,384]{2,1,0:T(8,128)(2,1)}, bf16[2,80,384]{2,1,0:T(8,128)(2,1)S(1)}, u32[]{:S(2)}, u32[]{:S(2)}) collective-permute-start(bf16[2,80,384]{2,1,0:T(8,128)(2,1)} %get-tuple-element.32), channel_id=1, source_target_pairs={{0,16},{1,17},{2,18},{3,19},{4,20},{5,21},{6,22},{7,23},{8,24},{9,... | collective-permute-start | bytes 368648 | tf_op jit(solution)/shard_map/ppermute | solution.py:71
  113.6 1.5 collective-permute-start.8
  115.2 5.2 %collective-permute-start.9 = (bf16[432,104]{1,0:T(8,128)(2,1)S(1)}, bf16[432,104]{1,0:T(8,128)(2,1)S(1)}, u32[]{:S(2)}, u32[]{:S(2)}) collective-permute-start(bf16[432,104]{1,0:T(8,128)(2,1)S(1)} %dynamic-slice_convert_fusion.1), channel_id=1, source_target_pairs={{0,2},{1,3},{2,0},{3,1},{4,6},{5,7},{6,4},{7,5},{8,10},{9,11},{10,... | collective-permute-start | bytes 269576 | tf_op jit(solution)/shard_map/ppermute | solution.py:71
  116.5 11.6 %collective-permute-start.17 = (bf16[2,160,384]{2,1,0:T(8,128)(2,1)S(1)}, bf16[2,160,384]{2,1,0:T(8,128)(2,1)S(1)}, u32[]{:S(2)}, u32[]{:S(2)}) collective-permute-start(bf16[2,160,384]{2,1,0:T(8,128)(2,1)S(1)} %pad_maximum_fusion.7), channel_id=1, source_target_pairs={{0,8},{1,9},{2,10},{3,11},{4,12},{5,13},{6,14},{7,15},{8,0},{9,1},... | collective-permute-start | bytes 737288 | tf_op jit(solution)/shard_map/ppermute | solution.py:71
  120.4 4.2 %collective-permute-start.10 = (bf16[216,104]{1,0:T(8,128)(2,1)S(1)}, bf16[216,104]{1,0:T(8,128)(2,1)S(1)}, u32[]{:S(2)}, u32[]{:S(2)}) collective-permute-start(bf16[216,104]{1,0:T(8,128)(2,1)S(1)} %dynamic-slice_convert_fusion.2), channel_id=1, source_target_pairs={{0,4},{1,5},{2,6},{3,7},{4,0},{5,1},{6,2},{7,3},{8,12},{9,13},{10,... | collective-permute-start | bytes 134792 | tf_op jit(solution)/shard_map/ppermute | solution.py:71
  124.7 5.6 %collective-permute-start.11 = (bf16[216,104]{1,0:T(8,128)(2,1)S(1)}, bf16[216,104]{1,0:T(8,128)(2,1)S(1)}, u32[]{:S(2)}, u32[]{:S(2)}) collective-permute-start(bf16[216,104]{1,0:T(8,128)(2,1)S(1)} %add_convert_fusion.2), channel_id=1, source_target_pairs={{0,8},{1,9},{2,10},{3,11},{4,12},{5,13},{6,14},{7,15},{8,0},{9,1},... | collective-permute-start | bytes 134792 | tf_op jit(solution)/shard_map/ppermute | solution.py:71
  128.2 6.3 %collective-permute-start.21 = (bf16[320,384]{1,0:T(8,128)(2,1)S(1)}, bf16[320,384]{1,0:T(8,128)(2,1)S(1)}, u32[]{:S(2)}, u32[]{:S(2)}) collective-permute-start(bf16[320,384]{1,0:T(8,128)(2,1)S(1)} %pad_maximum_fusion.9), channel_id=1, source_target_pairs={{0,2},{1,3},{2,0},{3,1},{4,6},{5,7},{6,4},{7,5},{8,10},{9,11},{10,... | collective-permute-start | bytes 737288 | tf_op jit(solution)/shard_map/ppermute | solution.py:71
  128.8 7.2 %collective-permute-start.18 = (bf16[320,384]{1,0:T(8,128)(2,1)S(1)}, bf16[320,384]{1,0:T(8,128)(2,1)S(1)}, u32[]{:S(2)}, u32[]{:S(2)}) collective-permute-start(bf16[320,384]{1,0:T(8,128)(2,1)S(1)} %pad_maximum_fusion.8), channel_id=1, source_target_pairs={{0,4},{1,5},{2,6},{3,7},{4,0},{5,1},{6,2},{7,3},{8,12},{9,13},{10,... | collective-permute-start | bytes 737288 | tf_op jit(solution)/shard_map/ppermute | solution.py:71
  130.2 16.2 %collective-permute-start.12 = (bf16[216,104]{1,0:T(8,128)(2,1)S(1)}, bf16[216,104]{1,0:T(8,128)(2,1)S(1)}, u32[]{:S(2)}, u32[]{:S(2)}) collective-permute-start(bf16[216,104]{1,0:T(8,128)(2,1)S(1)} %add_convert_fusion.1), channel_id=1, source_target_pairs={{0,16},{1,17},{2,18},{3,19},{4,20},{5,21},{6,22},{7,23},{8,24},{9,... | collective-permute-start | bytes 134792 | tf_op jit(solution)/shard_map/ppermute | solution.py:71
  134.5 11.1 %collective-permute-start.22 = (bf16[640,384]{1,0:T(8,128)(2,1)S(1)}, bf16[640,384]{1,0:T(8,128)(2,1)S(1)}, u32[]{:S(2)}, u32[]{:S(2)}) collective-permute-start(bf16[640,384]{1,0:T(8,128)(2,1)S(1)} %pad_maximum_fusion.4), channel_id=1, source_target_pairs={{0,4},{1,5},{2,6},{3,7},{4,0},{5,1},{6,2},{7,3},{8,12},{9,13},{10,... | collective-permute-start | bytes 1474568 | tf_op jit(solution)/shard_map/ppermute | solution.py:71
  136.0 9.7 %collective-permute-start.19 = (bf16[640,384]{1,0:T(8,128)(2,1)S(1)}, bf16[640,384]{1,0:T(8,128)(2,1)S(1)}, u32[]{:S(2)}, u32[]{:S(2)}) collective-permute-start(bf16[640,384]{1,0:T(8,128)(2,1)S(1)} %pad_maximum_fusion.3), channel_id=1, source_target_pairs={{0,2},{1,3},{2,0},{3,1},{4,6},{5,7},{6,4},{7,5},{8,10},{9,11},{10,... | collective-permute-start | bytes 1474568 | tf_op jit(solution)/shard_map/ppermute | solution.py:71
  145.7 11.3 %copy-start.7 = (bf16[1280,384]{1,0:T(8,128)(2,1)}, bf16[1280,384]{1,0:T(8,128)(2,1)S(1)}, u32[]{:S(2)}) copy-start(bf16[1280,384]{1,0:T(8,128)(2,1)S(1)} %constant_dynamic-update-slice_fusion.5.g10_ref) | copy-start | bytes 2949124
  145.7 11.3 %collective-permute-start.23 = (bf16[1280,384]{1,0:T(8,128)(2,1)S(1)}, bf16[1280,384]{1,0:T(8,128)(2,1)S(1)}, u32[]{:S(2)}, u32[]{:S(2)}) collective-permute-start(bf16[1280,384]{1,0:T(8,128)(2,1)S(1)} %constant_dynamic-update-slice_fusion.5.g10_ref), channel_id=1, source_target_pairs={{0,1},{1,0},{2,3},{3,2},{4,5},{5,4},{6,7},{7,6},{8,9},{9,8},{10,11... | collective-permute-start | bytes 2949128 | tf_op jit(solution)/shard_map/ppermute | solution.py:71
  145.9 11.1 %copy-start.8 = (bf16[1280,384]{1,0:T(8,128)(2,1)}, bf16[1280,384]{1,0:T(8,128)(2,1)S(1)}, u32[]{:S(2)}) copy-start(bf16[1280,384]{1,0:T(8,128)(2,1)S(1)} %constant_dynamic-update-slice_fusion.g00_ref) | copy-start | bytes 2949124
  145.9 11.1 %collective-permute-start.20 = (bf16[1280,384]{1,0:T(8,128)(2,1)S(1)}, bf16[1280,384]{1,0:T(8,128)(2,1)}, u32[]{:S(2)}, u32[]{:S(2)}) collective-permute-start(bf16[1280,384]{1,0:T(8,128)(2,1)S(1)} %constant_dynamic-update-slice_fusion.g00_ref), channel_id=1, source_target_pairs={{0,1},{1,0},{2,3},{3,2},{4,5},{5,4},{6,7},{7,6},{8,9},{9,8},{10,11... | collective-permute-start | bytes 2949128 | tf_op jit(solution)/shard_map/ppermute | solution.py:71
  146.4 4.2 %collective-permute-start.13 = (bf16[216,104]{1,0:T(8,128)(2,1)S(1)}, bf16[216,104]{1,0:T(8,128)(2,1)S(1)}, u32[]{:S(2)}, u32[]{:S(2)}) collective-permute-start(bf16[216,104]{1,0:T(8,128)(2,1)S(1)} %add_convert_fusion), channel_id=1, source_target_pairs={{0,4},{1,5},{2,6},{3,7},{4,0},{5,1},{6,2},{7,3},{8,12},{9,13},{10,... | collective-permute-start | bytes 134792 | tf_op jit(solution)/shard_map/ppermute | solution.py:71
  150.7 4.8 %collective-permute-start.14 = (bf16[432,104]{1,0:T(8,128)(2,1)S(1)}, bf16[432,104]{1,0:T(8,128)(2,1)S(1)}, u32[]{:S(2)}, u32[]{:S(2)}) collective-permute-start(bf16[432,104]{1,0:T(8,128)(2,1)S(1)} %maximum_select_fusion.3), channel_id=1, source_target_pairs={{0,2},{1,3},{2,0},{3,1},{4,6},{5,7},{6,4},{7,5},{8,10},{9,11},{10,... | collective-permute-start | bytes 269576 | tf_op jit(solution)/shard_map/ppermute | solution.py:71
  155.6 25.7 %collective-permute-start.15 = (bf16[864,104]{1,0:T(8,128)(2,1)S(1)}, bf16[864,104]{1,0:T(8,128)(2,1)S(1)}, u32[]{:S(2)}, u32[]{:S(2)}) collective-permute-start(bf16[864,104]{1,0:T(8,128)(2,1)S(1)} %maximum_select_fusion.2), channel_id=1, source_target_pairs={{0,1},{1,0},{2,3},{3,2},{4,5},{5,4},{6,7},{7,6},{8,9},{9,8},{10,11... | collective-permute-start | bytes 539144 | tf_op jit(solution)/shard_map/ppermute | solution.py:71
  175.5 4.7 %collective-permute-start.24 = (f32[128,32]{1,0:T(8,128)}, f32[128,32]{1,0:T(8,128)S(1)}, u32[]{:S(2)}, u32[]{:S(2)}) collective-permute-start(f32[128,32]{1,0:T(8,128)} %shard_map.131), channel_id=1, source_target_pairs={{0,4},{1,5},{2,6},{3,7},{4,0},{5,1},{6,2},{7,3},{8,12},{9,13},{10,... | collective-permute-start | bytes 49160 | tf_op jit(solution)/shard_map/ppermute | solution.py:71
  181.0 4.3 %collective-permute-start.25 = (f32[128,32]{1,0:T(8,128)S(1)}, f32[128,32]{1,0:T(8,128)S(1)}, u32[]{:S(2)}, u32[]{:S(2)}) collective-permute-start(f32[128,32]{1,0:T(8,128)S(1)} %add.203), channel_id=1, source_target_pairs={{0,8},{1,9},{2,10},{3,11},{4,12},{5,13},{6,14},{7,15},{8,0},{9,1},... | collective-permute-start | bytes 49160 | tf_op jit(solution)/shard_map/ppermute | solution.py:71
  185.4 5.6 %collective-permute-start.26 = (f32[128,32]{1,0:T(8,128)S(1)}, f32[128,32]{1,0:T(8,128)S(1)}, u32[]{:S(2)}, u32[]{:S(2)}) collective-permute-start(f32[128,32]{1,0:T(8,128)S(1)} %add.204), channel_id=1, source_target_pairs={{0,16},{1,17},{2,18},{3,19},{4,20},{5,21},{6,22},{7,23},{8,24},{9,... | collective-permute-start | bytes 49160 | tf_op jit(solution)/shard_map/ppermute | solution.py:71
  (11 other events, 31.0 us)

commit v3 on v2

--- a/solution.py
+++ b/solution.py
@@ -8,6 +8,7 @@
 from jax.experimental import pallas as pl
 from jax.experimental.pallas import tpu as pltpu
 from jax.sharding import PartitionSpec as P
+
 
 f32 = jnp.float32
 bf16 = jnp.bfloat16
@@ -46,11 +47,11 @@
         if self.halvings > 2:
             second[1], second[2] = second[2], second[1]
         self.orders = (first, second)
+        self.early = tuple([order[1], order[0]] + order[2:] for order in self.orders)
         self.rest = list(range(self.halvings, bits))
         self.turns = [[turn] for turn in range(self.halvings)]
 
-    def flips(self, color):
-        order = self.orders[color]
+    def flips(self, order):
         masks = []
         for relative in range(self.owners):
             mask = 0
@@ -74,16 +75,28 @@
         return self.trade(value, 1 << bit)
 
 
-def first_exchange(plan, keep, send):
-    if plan.halvings == 0:
-        return keep
-    return keep + plan.swap(send, plan.orders[0][0]).astype(f32)
+def two_exchanges(plan, orders, keep, *sends):
+    middle = keep.shape[0] // 2
+    keeps = [keep[:middle], keep[middle:]]
+    for turn in range(2):
+        bits = [order[turn] for order in orders]
+        if turn > 0:
+            middle = middle // 2
+            sends = [total[middle:].astype(bf16) for total in keeps]
+            keeps = [total[:middle] for total in keeps]
+        if bits[0] == bits[1] and turn > 0:
+            both = plan.swap(jnp.concatenate(sends, axis=0), bits[0])
+            arrived = [both[:middle], both[middle:]]
+        else:
+            arrived = [plan.swap(part, bit) for part, bit in zip(sends, bits)]
+        keeps = [part + other.astype(f32) for part, other in zip(keeps, arrived)]
+    return keeps
 
 
 def reduce_scatter(plan, fields, late):
     keeps = [jnp.stack([field[color] for field in fields]) for color in range(2)]
     arrived = []
-    for turn in range(1, len(plan.turns)):
+    for turn in range(2, len(plan.turns)):
         keeps = [sum([other[color].astype(f32) for other in arrived], keeps[color]) for color in range(2)]
         if turn == 2:
             keeps, late = lax.optimization_barrier((keeps, late))
@@ -122,14 +135,16 @@
                 both = jnp.stack(values)
                 others = [plan.trade(both, mask) for mask in masks[0]]
                 continue
+            if turn == 0:
+                values = lax.optimization_barrier(values)
             others = list(zip(*[[plan.trade(values[color], mask) for mask in masks[color]] for color in range(2)]))
     return [values[0], others[0][0], values[1], others[0][1]]
 
 
-def column_tables(plan, kept, rows_here, height, me, shard):
+def column_tables(plan, orders, kept, rows_here, height, me, shard):
     owner = me & (plan.owners - 1)
     heights = shard * rows_here + jnp.arange(rows_here, dtype=jnp.int32)
-    flips = jnp.asarray(np.stack([plan.flips(0), plan.flips(1)]))
+    flips = jnp.asarray(np.stack([plan.flips(order) for order in orders]))
     owned = jnp.bitwise_xor(owner, flips)
     ordinal = jnp.arange(plan.per, dtype=jnp.int32)[None, :, None] * plan.owners + owned[:, None, :]
     ordinal = ordinal.reshape(2, kept)
@@ -156,7 +171,7 @@
 
 
 def forward_kernel(
-    x_ref, table_ref, factor_ref, forth_ref, rows_ref, keep_ref, send_ref,
+    x_ref, table_ref, factor_ref, forth_ref, rows_ref, keep_ref, send0_ref, send1_ref,
     raw, projected, packed, *, plan, rank, rows_here,
 ):
     step = pl.program_id(0)
@@ -223,10 +238,10 @@
 
         middle = keep_ref.shape[0] // 2
         for t in range(tiles):
-            for color in range(2):
+            for color, send_ref in enumerate((send0_ref, send1_ref)):
                 here, start = slice(color * middle, (color + 1) * middle), 2 * color * middle
                 keep_ref[here, t * LANE : (t + 1) * LANE] = packed[t, start : start + middle]
-                send_ref[here, t * LANE : (t + 1) * LANE] = packed[t, start + middle : start + 2 * middle].astype(bf16)
+                send_ref[:, t * LANE : (t + 1) * LANE] = packed[t, start + middle : start + 2 * middle].astype(bf16)
 
 
 def forward(plan, field, table, factor, forth, rank, modes):
@@ -250,11 +265,12 @@
         out_specs=[
             pl.BlockSpec((channels, block * lanes), lambda s: (0, s)),
         ]
-        + [pl.BlockSpec((2 * middle, lanes), lambda s: (0, 0))] * 2,
+        + [pl.BlockSpec((rows, lanes), lambda s: (0, 0)) for rows in (2 * middle, middle, middle)],
         out_shape=[
             jax.ShapeDtypeStruct((channels, rows_here * lanes), bf16),
         ]
-        + [jax.ShapeDtypeStruct((2 * middle, lanes), dtype) for dtype in (f32, bf16)],
+        + [jax.ShapeDtypeStruct((2 * middle, lanes), f32)]
+        + [jax.ShapeDtypeStruct((middle, lanes), bf16)] * 2,
         scratch_shapes=[
             pltpu.VMEM((batch * table.shape[2] // LANE, channels * (block + 8), LANE), f32),
             pltpu.VMEM((lanes // LANE, rank_pad * (rows_here + 8), LANE), f32),
@@ -558,20 +574,17 @@
     me = shard * blocks + lax.axis_index("ch")
     plan = Plan(shards * blocks, kept)
     table = row_tables(batch, width, modes)
-    forth, back = column_tables(plan, kept, rows_here, rows_here * shards, me, shard)
+    early, _ = column_tables(plan, plan.early, kept, rows_here, rows_here * shards, me, shard)
+    forth, back = column_tables(plan, plan.orders, kept, rows_here, rows_here * shards, me, shard)
 
     def padded(factor):
         rank = factor.shape[1]
         return jnp.pad(factor.T, ((0, round_up(rank, 8) - rank), (0, 0)))
 
-    def exchanged(parts):
-        total = first_exchange(plan, *parts)
-        return total.reshape(2, total.shape[0] // 2, total.shape[1])
-
-    rows_input, *left = forward(plan, inputs, table, padded(input_factor), forth, rank_in, modes)
-    left = exchanged(left)
+    rows_input, *left = forward(plan, inputs, table, padded(input_factor), early, rank_in, modes)
+    left = two_exchanges(plan, plan.early, *left)
     rows_cot, *right = forward(plan, cotangent, table, padded(output_factor), forth, rank_out, modes)
-    right = exchanged(right)
+    right = two_exchanges(plan, plan.orders, *right)
     keep, arrived, (core_tensor, height_factor, width_factor) = reduce_scatter(
         plan, (left, right), (core_tensor, height_factor, width_factor)
     )

time: 193 us -> 205 us (1.062)
  waiting for transfers between devices: 53.5 us -> 64.7 us
  starting transfers between devices: 31.5 us -> 28.4 us
  local copies, waits for them, and re-layouts: 19.8 us -> 22 us
    ppermute x27 -> x30, waiting for transfers between devices: 53.5 us -> 64.7 us  [trade(): return lax.ppermute(value, AXES, [(i, i ^ mask) for i in range(self.total)])]
    ppermute x27 -> x30, starting transfers between devices: 31.5 us -> 28.4 us  [trade(): return lax.ppermute(value, AXES, [(i, i ^ mask) for i in range(self.total)])]
  transfers between devices with their start and end apart: 27 -> 30, of which waited for: 18 -> 19; matrix products, arithmetic and copies ran while one was open for 12% -> 13% of each run, Pallas kernels for 22% -> 21%
where the time goes in v3:
time: 205 us; the launch traced here: 204 us
  Pallas kernels  73.7 us (36%)
  waiting for transfers between devices  64.7 us (32%)
  starting transfers between devices  28.4 us (14%)
  local copies, waits for them, and re-layouts  22 us (11%)
  other arithmetic  13.4 us (7%)
    ppermute x30, waiting for transfers between devices, trade(): return lax.ppermute(value, AXES, [(i, i ^ mask) for i in range(self.total)])  64.7 us
    pallas_call x2, Pallas kernels, forward(): pl.pallas_call(functools.partial(forward_kernel, plan=plan, rank=rank, ro...  48.7 us
    ppermute x30, starting transfers between devices, trade(): return lax.ppermute(value, AXES, [(i, i ^ mask) for i in range(self.total)])  28.4 us
    pallas_call x1, Pallas kernels, backward(): pl.pallas_call(functools.partial(backward_kernel, plan=plan, ranks=ranks,...  17.6 us
    pallas_call x1, Pallas kernels, owner_work(): pl.pallas_call(functools.partial(owner_kernel, plan=plan, batch=batch, ra...  7.39 us
  transfers between devices with their start and end apart: 30, of which 19 were waited for; matrix products, arithmetic and copies ran while one was open for 13% of the time, Pallas kernels for 21%

profile of v3, /device:TPU:0, one launch (start us, length us, event | category | flops | bytes accessed | tf_op | source)
XLA Modules:
  0.0 203.5 jit_solution(4558940324342447102)
XLA Ops:
  3.2 1.3 pad.38.factor_ref
  4.5 24.3 %shard_map.138 = (bf16[64,49152]{1,0:T(8,128)(2,1)}, f32[1280,384]{1,0:T(8,128)}, bf16[640,384]{1,0:T(8,128)(2,1)}, bf16[640,384]{1,0:T(8,128)(2,1)}) custom-call(bf16[2,64,128,1024]{3,2,1,0:T(8,128)(2,1)} %x_ref.3, bf16[2,1024,256]{2,1,0:T(8,128)(2,1)} %constant.104.table_ref, bf16[32,64]{1,0:T(8,128)(2,1)} %pad.38.factor_ref, ...), custom_call_target="tpu_custom_call" | custom-call | flops 6442450944 | bytes 39845888 | tf_op jit(solution)/shard_map/pallas_call | solution.py:256
  30.7 24.4 %shard_map.137 = (bf16[64,49152]{1,0:T(8,128)(2,1)}, f32[1280,384]{1,0:T(8,128)}, bf16[640,384]{1,0:T(8,128)(2,1)}, bf16[640,384]{1,0:T(8,128)(2,1)}) custom-call(bf16[2,64,128,1024]{3,2,1,0:T(8,128)(2,1)} %x_ref.2, bf16[2,1024,256]{2,1,0:T(8,128)(2,1)} %constant.104.table_ref, bf16[32,64]{1,0:T(8,128)(2,1)} %pad.37.factor_ref, ...), custom_call_target="tpu_custom_call" | custom-call | flops 6442450944 | bytes 39845888 | tf_op jit(solution)/shard_map/pallas_call | solution.py:256
  55.1 2.9 %collective-permute-start = (bf16[640,384]{1,0:T(8,128)(2,1)}, bf16[640,384]{1,0:T(8,128)(2,1)S(1)}, u32[]{:S(2)}, u32[]{:S(2)}) collective-permute-start(bf16[640,384]{1,0:T(8,128)(2,1)} %get-tuple-element.25), channel_id=1, source_target_pairs={{0,2},{1,3},{2,0},{3,1},{4,6},{5,7},{6,4},{7,5},{8,10},{9,11},{10,... | collective-permute-start | bytes 1474568 | tf_op jit(solution)/shard_map/ppermute | solution.py:72
  58.0 1.5 collective-permute-start.1
  60.4 9.3 %collective-permute-done = bf16[640,384]{1,0:T(8,128)(2,1)S(1)} collective-permute-done((bf16[640,384]{1,0:T(8,128)(2,1)}, bf16[640,384]{1,0:T(8,128)(2,1)S(1)}, u32[]{:S(2)}, u32[]{:S(2)}) %collective-permute-start) | collective-permute-done | bytes 491552 | tf_op jit(solution)/shard_map/ppermute | solution.py:72
  69.7 2.7 %collective-permute-done.1 = bf16[640,384]{1,0:T(8,128)(2,1)} collective-permute-done((bf16[640,384]{1,0:T(8,128)(2,1)}, bf16[640,384]{1,0:T(8,128)(2,1)}, u32[]{:S(2)}, u32[]{:S(2)}) %collective-permute-start.1) | collective-permute-done | bytes 491552 | tf_op jit(solution)/shard_map/ppermute | solution.py:72
  74.1 2.3 %collective-permute-done.6 = bf16[320,384]{1,0:T(8,128)(2,1)S(1)} collective-permute-done((bf16[320,384]{1,0:T(8,128)(2,1)S(1)}, bf16[320,384]{1,0:T(8,128)(2,1)S(1)}, u32[]{:S(2)}, u32[]{:S(2)}) %collective-permute-start.6) | collective-permute-done | bytes 245792 | tf_op jit(solution)/shard_map/ppermute | solution.py:72
  76.4 5.9 %collective-permute-done.4 = bf16[320,384]{1,0:T(8,128)(2,1)S(1)} collective-permute-done((bf16[320,384]{1,0:T(8,128)(2,1)S(1)}, bf16[320,384]{1,0:T(8,128)(2,1)S(1)}, u32[]{:S(2)}, u32[]{:S(2)}) %collective-permute-start.4) | collective-permute-done | bytes 245792 | tf_op jit(solution)/shard_map/ppermute | solution.py:72
  85.3 1.8 collective-permute-start.7
  88.6 3.4 %copy.22 = f32[2,26,26,100]{3,2,1,0:T(8,128)S(1)} copy(f32[2,26,26,100]{2,0,3,1:T(2,128)} %bitcast.81) | data formatting | bytes 1081600 | tf_op jit(solution)/shard_map/reshape | solution.py:496
  95.6 1.6 collective-permute-start.9
  100.0 2.6 %collective-permute-done.9 = bf16[2,2,80,384]{3,2,1,0:T(8,128)(2,1)S(1)} collective-permute-done((bf16[2,2,80,384]{3,2,1,0:T(8,128)(2,1)S(1)}, bf16[2,2,80,384]{3,2,1,0:T(8,128)(2,1)S(1)}, u32[]{:S(2)}, u32[]{:S(2)}) %collective-permute-start.9) | collective-permute-done | bytes 245792 | tf_op jit(solution)/shard_map/ppermute | solution.py:72
  102.7 2.7 %collective-permute-start.10 = (bf16[2,2,40,384]{3,2,1,0:T(8,128)(2,1)S(1)}, bf16[2,2,40,384]{3,2,1,0:T(8,128)(2,1)S(1)}, u32[]{:S(2)}, u32[]{:S(2)}) collective-permute-start(bf16[2,2,40,384]{3,2,1,0:T(8,128)(2,1)S(1)} %pad_maximum_fusion.12), channel_id=1, source_target_pairs={{0,16},{1,17},{2,18},{3,19},{4,20},{5,21},{6,22},{7,23},{8,24},{9,... | collective-permute-start | bytes 368648 | tf_op jit(solution)/shard_map/ppermute | solution.py:72
  106.1 3.8 %collective-permute-done.10.refs_0_ = bf16[2,2,40,384]{3,2,1,0:T(8,128)(2,1)S(1)} collective-permute-done((bf16[2,2,40,384]{3,2,1,0:T(8,128)(2,1)S(1)}, bf16[2,2,40,384]{3,2,1,0:T(8,128)(2,1)S(1)}, u32[]{:S(2)}, u32[]{:S(2)}) %collective-permute-start.10) | collective-permute-done | bytes 122912 | tf_op jit(solution)/shard_map/ppermute | solution.py:72
  110.5 7.4 %shard_map.139 = (f32[1664,104]{1,0:T(8,128)}, f32[3,104,1]{2,1,0:T(8,128)}, f32[104,128]{1,0:T(8,128)}, bf16[2,80,384]{2,1,0:T(8,128)(2,1)}) custom-call(f32[2,2,40,384]{3,2,1,0:T(8,128)} %pad_maximum_fusion.7.keep_ref, bf16[2,1664,104]{2,1,0:T(8,128)(2,1)} %copy.27.core_ref, bf16[2,104,1664]{2,1,0:T(8,128)(2,1)} %get-tuple-element.59.core_t_ref, ...), custom_call_target="tpu_custom_call" | custom-call | tf_op jit(solution)/shard_map/pallas_call | solution.py:507
  117.9 1.4 collective-permute-start.19
  125.5 2.2 %collective-permute-start.12 = (bf16[432,104]{1,0:T(8,128)(2,1)S(1)}, bf16[432,104]{1,0:T(8,128)(2,1)S(1)}, u32[]{:S(2)}, u32[]{:S(2)}) collective-permute-start(bf16[432,104]{1,0:T(8,128)(2,1)S(1)} %dynamic-slice_convert_fusion.1), channel_id=1, source_target_pairs={{0,2},{1,3},{2,0},{3,1},{4,6},{5,7},{6,4},{7,5},{8,10},{9,11},{10,... | collective-permute-start | bytes 269576 | tf_op jit(solution)/shard_map/ppermute | solution.py:72
  127.8 2.7 %collective-permute-start.20 = (bf16[2,160,384]{2,1,0:T(8,128)(2,1)S(1)}, bf16[2,160,384]{2,1,0:T(8,128)(2,1)S(1)}, u32[]{:S(2)}, u32[]{:S(2)}) collective-permute-start(bf16[2,160,384]{2,1,0:T(8,128)(2,1)S(1)} %pad_maximum_fusion.8), channel_id=1, source_target_pairs={{0,8},{1,9},{2,10},{3,11},{4,12},{5,13},{6,14},{7,15},{8,0},{9,1},... | collective-permute-start | bytes 737288 | tf_op jit(solution)/shard_map/ppermute | solution.py:72
  132.0 3.4 %collective-permute-done.13 = bf16[216,104]{1,0:T(8,128)(2,1)S(1)} collective-permute-done((bf16[216,104]{1,0:T(8,128)(2,1)S(1)}, bf16[216,104]{1,0:T(8,128)(2,1)S(1)}, u32[]{:S(2)}, u32[]{:S(2)}) %collective-permute-start.13) | collective-permute-done | bytes 44960 | tf_op jit(solution)/shard_map/ppermute | solution.py:72
  135.4 3.0 %collective-permute-start.14 = (bf16[216,104]{1,0:T(8,128)(2,1)S(1)}, bf16[216,104]{1,0:T(8,128)(2,1)S(1)}, u32[]{:S(2)}, u32[]{:S(2)}) collective-permute-start(bf16[216,104]{1,0:T(8,128)(2,1)S(1)} %add_convert_fusion.2), channel_id=1, source_target_pairs={{0,8},{1,9},{2,10},{3,11},{4,12},{5,13},{6,14},{7,15},{8,0},{9,1},... | collective-permute-start | bytes 134792 | tf_op jit(solution)/shard_map/ppermute | solution.py:72
  138.4 1.6 collective-permute-start.23
  141.5 3.2 %collective-permute-done.23 = bf16[320,384]{1,0:T(8,128)(2,1)S(1)} collective-permute-done((bf16[320,384]{1,0:T(8,128)(2,1)S(1)}, bf16[320,384]{1,0:T(8,128)(2,1)S(1)}, u32[]{:S(2)}, u32[]{:S(2)}) %collective-permute-start.23) | collective-permute-done | bytes 245792 | tf_op jit(solution)/shard_map/ppermute | solution.py:72
  145.3 2.8 %collective-permute-done.21 = bf16[320,384]{1,0:T(8,128)(2,1)S(1)} collective-permute-done((bf16[320,384]{1,0:T(8,128)(2,1)S(1)}, bf16[320,384]{1,0:T(8,128)(2,1)S(1)}, u32[]{:S(2)}, u32[]{:S(2)}) %collective-permute-start.21) | collective-permute-done | bytes 245792 | tf_op jit(solution)/shard_map/ppermute | solution.py:72
  148.4 8.4 %collective-permute-done.24 = bf16[640,384]{1,0:T(8,128)(2,1)S(1)} collective-permute-done((bf16[640,384]{1,0:T(8,128)(2,1)S(1)}, bf16[640,384]{1,0:T(8,128)(2,1)S(1)}, u32[]{:S(2)}, u32[]{:S(2)}) %collective-permute-start.24) | collective-permute-done | bytes 491552 | tf_op jit(solution)/shard_map/ppermute | solution.py:72
  158.4 3.6 %collective-permute-done.16 = bf16[216,104]{1,0:T(8,128)(2,1)S(1)} collective-permute-done((bf16[216,104]{1,0:T(8,128)(2,1)S(1)}, bf16[216,104]{1,0:T(8,128)(2,1)S(1)}, u32[]{:S(2)}, u32[]{:S(2)}) %collective-permute-start.16) | collective-permute-done | bytes 44960 | tf_op jit(solution)/shard_map/ppermute | solution.py:72
  162.5 4.4 %collective-permute-done.17 = bf16[432,104]{1,0:T(8,128)(2,1)S(1)} collective-permute-done((bf16[432,104]{1,0:T(8,128)(2,1)S(1)}, bf16[432,104]{1,0:T(8,128)(2,1)S(1)}, u32[]{:S(2)}, u32[]{:S(2)}) %collective-permute-start.17) | collective-permute-done | bytes 89888 | tf_op jit(solution)/shard_map/ppermute | solution.py:72
  169.3 17.6 %shard_map.140 = f32[128,32]{1,0:T(8,128)} custom-call(bf16[1280,384]{1,0:T(8,128)(2,1)} %copy-done.5, bf16[1280,384]{1,0:T(8,128)(2,1)} %copy-done.6, bf16[1280,384]{1,0:T(8,128)(2,1)} %copy-done.4, bf16[1280,384]{1,0:T(8,128)(2,1)} %collective-permute-done.26.g11_ref, bf16[64,49152]{1,0:T(8,128)(2,1)} %get-tuple-element.41.rows_in_ref, ...), custom_call_target="tpu_custom_call" | custom-call | flops 402653184 | bytes 12582912 | tf_op jit(solution)/shard_map/pallas_call | solution.py:360
  187.4 4.2 %collective-permute-done.27 = f32[128,32]{1,0:T(8,128)S(1)} collective-permute-done((f32[128,32]{1,0:T(8,128)}, f32[128,32]{1,0:T(8,128)S(1)}, u32[]{:S(2)}, u32[]{:S(2)}) %collective-permute-start.27) | collective-permute-done | bytes 16416 | tf_op jit(solution)/shard_map/ppermute | solution.py:72
  192.6 4.1 %collective-permute-done.28 = f32[128,32]{1,0:T(8,128)S(1)} collective-permute-done((f32[128,32]{1,0:T(8,128)S(1)}, f32[128,32]{1,0:T(8,128)S(1)}, u32[]{:S(2)}, u32[]{:S(2)}) %collective-permute-start.28) | collective-permute-done | bytes 16416 | tf_op jit(solution)/shard_map/ppermute | solution.py:72
  197.6 2.8 %copy.29 = f32[2,26,26,100]{2,0,3,1:T(2,128)} copy(f32[2,26,26,100]{3,2,1,0:T(8,128)S(1)} %bitcast.80) | data formatting | bytes 1081600 | tf_op jit(solution)/shard_map/slice | solution.py:614
  200.3 1.8 collective-permute-done.29
  (169 shorter events, 37.1 us)
Async XLA Ops:
  4.5 24.9 %copy-start.12 = (bf16[64,26]{0,1:T(8,128)(2,1)S(1)}, bf16[64,26]{0,1:T(8,128)(2,1)}, u32[]{:S(2)}) copy-start(bf16[64,26]{0,1:T(8,128)(2,1)} %param.12) | copy-start | bytes 9988
  28.9 30.7 %collective-permute-start.3 = (bf16[640,384]{1,0:T(8,128)(2,1)}, bf16[640,384]{1,0:T(8,128)(2,1)S(1)}, u32[]{:S(2)}, u32[]{:S(2)}) collective-permute-start(bf16[640,384]{1,0:T(8,128)(2,1)} %get-tuple-element.28), channel_id=1, source_target_pairs={{0,1},{1,0},{2,3},{3,2},{4,5},{5,4},{6,7},{7,6},{8,9},{9,8},{10,11... | collective-permute-start | bytes 1474568 | tf_op jit(solution)/shard_map/ppermute | solution.py:72
  29.4 30.2 %collective-permute-start.5 = (bf16[640,384]{1,0:T(8,128)(2,1)}, bf16[640,384]{1,0:T(8,128)(2,1)S(1)}, u32[]{:S(2)}, u32[]{:S(2)}) collective-permute-start(bf16[640,384]{1,0:T(8,128)(2,1)} %get-tuple-element.29), channel_id=1, source_target_pairs={{0,1},{1,0},{2,3},{3,2},{4,5},{5,4},{6,7},{7,6},{8,9},{9,8},{10,11... | collective-permute-start | bytes 1474568 | tf_op jit(solution)/shard_map/ppermute | solution.py:72
  30.7 28.9 %copy-start.2 = (f32[1280,384]{1,0:T(8,128)S(1)}, f32[1280,384]{1,0:T(8,128)}, u32[]{:S(2)}) copy-start(f32[1280,384]{1,0:T(8,128)} %get-tuple-element.27) | copy-start | bytes 5898244
  55.1 14.6 %collective-permute-start = (bf16[640,384]{1,0:T(8,128)(2,1)}, bf16[640,384]{1,0:T(8,128)(2,1)S(1)}, u32[]{:S(2)}, u32[]{:S(2)}) collective-permute-start(bf16[640,384]{1,0:T(8,128)(2,1)} %get-tuple-element.25), channel_id=1, source_target_pairs={{0,2},{1,3},{2,0},{3,1},{4,6},{5,7},{6,4},{7,5},{8,10},{9,11},{10,... | collective-permute-start | bytes 1474568 | tf_op jit(solution)/shard_map/ppermute | solution.py:72
  58.0 14.4 %collective-permute-start.1 = (bf16[640,384]{1,0:T(8,128)(2,1)}, bf16[640,384]{1,0:T(8,128)(2,1)}, u32[]{:S(2)}, u32[]{:S(2)}) collective-permute-start(bf16[640,384]{1,0:T(8,128)(2,1)} %get-tuple-element.26), channel_id=1, source_target_pairs={{0,4},{1,5},{2,6},{3,7},{4,0},{5,1},{6,2},{7,3},{8,12},{9,13},{10,... | collective-permute-start | bytes 1474568 | tf_op jit(solution)/shard_map/ppermute | solution.py:72
  59.8 16.6 %collective-permute-start.6 = (bf16[320,384]{1,0:T(8,128)(2,1)S(1)}, bf16[320,384]{1,0:T(8,128)(2,1)S(1)}, u32[]{:S(2)}, u32[]{:S(2)}) collective-permute-start(bf16[320,384]{1,0:T(8,128)(2,1)S(1)} %slice.283), channel_id=1, source_target_pairs={{0,4},{1,5},{2,6},{3,7},{4,0},{5,1},{6,2},{7,3},{8,12},{9,13},{10,... | collective-permute-start | bytes 737288 | tf_op jit(solution)/shard_map/ppermute | solution.py:72
  73.8 8.6 %collective-permute-start.2 = (bf16[640,384]{1,0:T(8,128)(2,1)S(1)}, bf16[640,384]{1,0:T(8,128)(2,1)S(1)}, u32[]{:S(2)}, u32[]{:S(2)}) collective-permute-start(bf16[640,384]{1,0:T(8,128)(2,1)S(1)} %pad_maximum_fusion.3), channel_id=1, source_target_pairs={{0,1},{1,0},{2,3},{3,2},{4,5},{5,4},{6,7},{7,6},{8,9},{9,8},{10,11... | collective-permute-start | bytes 1474568 | tf_op jit(solution)/shard_map/ppermute | solution.py:72
  73.9 8.4 %collective-permute-start.4 = (bf16[320,384]{1,0:T(8,128)(2,1)S(1)}, bf16[320,384]{1,0:T(8,128)(2,1)S(1)}, u32[]{:S(2)}, u32[]{:S(2)}) collective-permute-start(bf16[320,384]{1,0:T(8,128)(2,1)S(1)} %slice.284), channel_id=1, source_target_pairs={{0,2},{1,3},{2,0},{3,1},{4,6},{5,7},{6,4},{7,5},{8,10},{9,11},{10,... | collective-permute-start | bytes 737288 | tf_op jit(solution)/shard_map/ppermute | solution.py:72
  84.3 9.2 %collective-permute-start.8 = (bf16[2,160,384]{2,1,0:T(8,128)(2,1)}, bf16[2,160,384]{2,1,0:T(8,128)(2,1)}, u32[]{:S(2)}, u32[]{:S(2)}) collective-permute-start(bf16[2,160,384]{2,1,0:T(8,128)(2,1)} %slice.281), channel_id=1, source_target_pairs={{0,2},{1,3},{2,0},{3,1},{4,6},{5,7},{6,4},{7,5},{8,10},{9,11},{10,... | collective-permute-start | bytes 737288 | tf_op jit(solution)/shard_map/ppermute | solution.py:72
  85.3 9.2 %collective-permute-start.7 = (bf16[2,160,384]{2,1,0:T(8,128)(2,1)}, bf16[2,160,384]{2,1,0:T(8,128)(2,1)}, u32[]{:S(2)}, u32[]{:S(2)}) collective-permute-start(bf16[2,160,384]{2,1,0:T(8,128)(2,1)} %slice.282), channel_id=1, source_target_pairs={{0,4},{1,5},{2,6},{3,7},{4,0},{5,1},{6,2},{7,3},{8,12},{9,13},{10,... | collective-permute-start | bytes 737288 | tf_op jit(solution)/shard_map/ppermute | solution.py:72
  95.6 7.0 %collective-permute-start.9 = (bf16[2,2,80,384]{3,2,1,0:T(8,128)(2,1)S(1)}, bf16[2,2,80,384]{3,2,1,0:T(8,128)(2,1)S(1)}, u32[]{:S(2)}, u32[]{:S(2)}) collective-permute-start(bf16[2,2,80,384]{3,2,1,0:T(8,128)(2,1)S(1)} %pad_maximum_fusion.6), channel_id=1, source_target_pairs={{0,8},{1,9},{2,10},{3,11},{4,12},{5,13},{6,14},{7,15},{8,0},{9,1},... | collective-permute-start | bytes 737288 | tf_op jit(solution)/shard_map/ppermute | solution.py:72
  102.7 7.2 %collective-permute-start.10 = (bf16[2,2,40,384]{3,2,1,0:T(8,128)(2,1)S(1)}, bf16[2,2,40,384]{3,2,1,0:T(8,128)(2,1)S(1)}, u32[]{:S(2)}, u32[]{:S(2)}) collective-permute-start(bf16[2,2,40,384]{3,2,1,0:T(8,128)(2,1)S(1)} %pad_maximum_fusion.12), channel_id=1, source_target_pairs={{0,16},{1,17},{2,18},{3,19},{4,20},{5,21},{6,22},{7,23},{8,24},{9,... | collective-permute-start | bytes 368648 | tf_op jit(solution)/shard_map/ppermute | solution.py:72
  117.9 7.3 %collective-permute-start.19 = (bf16[2,80,384]{2,1,0:T(8,128)(2,1)}, bf16[2,80,384]{2,1,0:T(8,128)(2,1)S(1)}, u32[]{:S(2)}, u32[]{:S(2)}) collective-permute-start(bf16[2,80,384]{2,1,0:T(8,128)(2,1)} %get-tuple-element.38), channel_id=1, source_target_pairs={{0,16},{1,17},{2,18},{3,19},{4,20},{5,21},{6,22},{7,23},{8,24},{9,... | collective-permute-start | bytes 368648 | tf_op jit(solution)/shard_map/ppermute | solution.py:72
  123.9 1.5 collective-permute-start.11
  125.5 5.6 %collective-permute-start.12 = (bf16[432,104]{1,0:T(8,128)(2,1)S(1)}, bf16[432,104]{1,0:T(8,128)(2,1)S(1)}, u32[]{:S(2)}, u32[]{:S(2)}) collective-permute-start(bf16[432,104]{1,0:T(8,128)(2,1)S(1)} %dynamic-slice_convert_fusion.1), channel_id=1, source_target_pairs={{0,2},{1,3},{2,0},{3,1},{4,6},{5,7},{6,4},{7,5},{8,10},{9,11},{10,... | collective-permute-start | bytes 269576 | tf_op jit(solution)/shard_map/ppermute | solution.py:72
  127.8 10.6 %collective-permute-start.20 = (bf16[2,160,384]{2,1,0:T(8,128)(2,1)S(1)}, bf16[2,160,384]{2,1,0:T(8,128)(2,1)S(1)}, u32[]{:S(2)}, u32[]{:S(2)}) collective-permute-start(bf16[2,160,384]{2,1,0:T(8,128)(2,1)S(1)} %pad_maximum_fusion.8), channel_id=1, source_target_pairs={{0,8},{1,9},{2,10},{3,11},{4,12},{5,13},{6,14},{7,15},{8,0},{9,1},... | collective-permute-start | bytes 737288 | tf_op jit(solution)/shard_map/ppermute | solution.py:72
  131.1 4.2 %collective-permute-start.13 = (bf16[216,104]{1,0:T(8,128)(2,1)S(1)}, bf16[216,104]{1,0:T(8,128)(2,1)S(1)}, u32[]{:S(2)}, u32[]{:S(2)}) collective-permute-start(bf16[216,104]{1,0:T(8,128)(2,1)S(1)} %dynamic-slice_convert_fusion.2), channel_id=1, source_target_pairs={{0,4},{1,5},{2,6},{3,7},{4,0},{5,1},{6,2},{7,3},{8,12},{9,13},{10,... | collective-permute-start | bytes 134792 | tf_op jit(solution)/shard_map/ppermute | solution.py:72
  135.4 5.2 %collective-permute-start.14 = (bf16[216,104]{1,0:T(8,128)(2,1)S(1)}, bf16[216,104]{1,0:T(8,128)(2,1)S(1)}, u32[]{:S(2)}, u32[]{:S(2)}) collective-permute-start(bf16[216,104]{1,0:T(8,128)(2,1)S(1)} %add_convert_fusion.2), channel_id=1, source_target_pairs={{0,8},{1,9},{2,10},{3,11},{4,12},{5,13},{6,14},{7,15},{8,0},{9,1},... | collective-permute-start | bytes 134792 | tf_op jit(solution)/shard_map/ppermute | solution.py:72
  138.4 6.3 %collective-permute-start.23 = (bf16[320,384]{1,0:T(8,128)(2,1)S(1)}, bf16[320,384]{1,0:T(8,128)(2,1)S(1)}, u32[]{:S(2)}, u32[]{:S(2)}) collective-permute-start(bf16[320,384]{1,0:T(8,128)(2,1)S(1)} %pad_maximum_fusion.10), channel_id=1, source_target_pairs={{0,2},{1,3},{2,0},{3,1},{4,6},{5,7},{6,4},{7,5},{8,10},{9,11},{10,... | collective-permute-start | bytes 737288 | tf_op jit(solution)/shard_map/ppermute | solution.py:72
  140.0 8.1 %collective-permute-start.21 = (bf16[320,384]{1,0:T(8,128)(2,1)S(1)}, bf16[320,384]{1,0:T(8,128)(2,1)S(1)}, u32[]{:S(2)}, u32[]{:S(2)}) collective-permute-start(bf16[320,384]{1,0:T(8,128)(2,1)S(1)} %pad_maximum_fusion.9), channel_id=1, source_target_pairs={{0,4},{1,5},{2,6},{3,7},{4,0},{5,1},{6,2},{7,3},{8,12},{9,13},{10,... | collective-permute-start | bytes 737288 | tf_op jit(solution)/shard_map/ppermute | solution.py:72
  140.6 17.2 %collective-permute-start.15 = (bf16[216,104]{1,0:T(8,128)(2,1)S(1)}, bf16[216,104]{1,0:T(8,128)(2,1)S(1)}, u32[]{:S(2)}, u32[]{:S(2)}) collective-permute-start(bf16[216,104]{1,0:T(8,128)(2,1)S(1)} %add_convert_fusion.1), channel_id=1, source_target_pairs={{0,16},{1,17},{2,18},{3,19},{4,20},{5,21},{6,22},{7,23},{8,24},{9,... | collective-permute-start | bytes 134792 | tf_op jit(solution)/shard_map/ppermute | solution.py:72
  144.8 12.1 %collective-permute-start.24 = (bf16[640,384]{1,0:T(8,128)(2,1)S(1)}, bf16[640,384]{1,0:T(8,128)(2,1)S(1)}, u32[]{:S(2)}, u32[]{:S(2)}) collective-permute-start(bf16[640,384]{1,0:T(8,128)(2,1)S(1)} %pad_maximum_fusion.5), channel_id=1, source_target_pairs={{0,4},{1,5},{2,6},{3,7},{4,0},{5,1},{6,2},{7,3},{8,12},{9,13},{10,... | collective-permute-start | bytes 1474568 | tf_op jit(solution)/shard_map/ppermute | solution.py:72
  148.2 8.9 %collective-permute-start.22 = (bf16[640,384]{1,0:T(8,128)(2,1)S(1)}, bf16[640,384]{1,0:T(8,128)(2,1)S(1)}, u32[]{:S(2)}, u32[]{:S(2)}) collective-permute-start(bf16[640,384]{1,0:T(8,128)(2,1)S(1)} %pad_maximum_fusion.4), channel_id=1, source_target_pairs={{0,2},{1,3},{2,0},{3,1},{4,6},{5,7},{6,4},{7,5},{8,10},{9,11},{10,... | collective-permute-start | bytes 1474568 | tf_op jit(solution)/shard_map/ppermute | solution.py:72
  157.2 11.1 %collective-permute-start.25 = (bf16[1280,384]{1,0:T(8,128)(2,1)S(1)}, bf16[1280,384]{1,0:T(8,128)(2,1)S(1)}, u32[]{:S(2)}, u32[]{:S(2)}) collective-permute-start(bf16[1280,384]{1,0:T(8,128)(2,1)S(1)} %constant_dynamic-update-slice_fusion.g00_ref), channel_id=1, source_target_pairs={{0,1},{1,0},{2,3},{3,2},{4,5},{5,4},{6,7},{7,6},{8,9},{9,8},{10,11... | collective-permute-start | bytes 2949128 | tf_op jit(solution)/shard_map/ppermute | solution.py:72
  157.3 11.0 %collective-permute-start.26 = (bf16[1280,384]{1,0:T(8,128)(2,1)S(1)}, bf16[1280,384]{1,0:T(8,128)(2,1)}, u32[]{:S(2)}, u32[]{:S(2)}) collective-permute-start(bf16[1280,384]{1,0:T(8,128)(2,1)S(1)} %constant_dynamic-update-slice_fusion.5.g10_ref), channel_id=1, source_target_pairs={{0,1},{1,0},{2,3},{3,2},{4,5},{5,4},{6,7},{7,6},{8,9},{9,8},{10,11... | collective-permute-start | bytes 2949128 | tf_op jit(solution)/shard_map/ppermute | solution.py:72
  157.8 4.2 %collective-permute-start.16 = (bf16[216,104]{1,0:T(8,128)(2,1)S(1)}, bf16[216,104]{1,0:T(8,128)(2,1)S(1)}, u32[]{:S(2)}, u32[]{:S(2)}) collective-permute-start(bf16[216,104]{1,0:T(8,128)(2,1)S(1)} %add_convert_fusion), channel_id=1, source_target_pairs={{0,4},{1,5},{2,6},{3,7},{4,0},{5,1},{6,2},{7,3},{8,12},{9,13},{10,... | collective-permute-start | bytes 134792 | tf_op jit(solution)/shard_map/ppermute | solution.py:72
  162.1 4.8 %collective-permute-start.17 = (bf16[432,104]{1,0:T(8,128)(2,1)S(1)}, bf16[432,104]{1,0:T(8,128)(2,1)S(1)}, u32[]{:S(2)}, u32[]{:S(2)}) collective-permute-start(bf16[432,104]{1,0:T(8,128)(2,1)S(1)} %maximum_select_fusion.3), channel_id=1, source_target_pairs={{0,2},{1,3},{2,0},{3,1},{4,6},{5,7},{6,4},{7,5},{8,10},{9,11},{10,... | collective-permute-start | bytes 269576 | tf_op jit(solution)/shard_map/ppermute | solution.py:72
  167.0 25.5 %collective-permute-start.18 = (bf16[864,104]{1,0:T(8,128)(2,1)S(1)}, bf16[864,104]{1,0:T(8,128)(2,1)S(1)}, u32[]{:S(2)}, u32[]{:S(2)}) collective-permute-start(bf16[864,104]{1,0:T(8,128)(2,1)S(1)} %maximum_select_fusion.2), channel_id=1, source_target_pairs={{0,1},{1,0},{2,3},{3,2},{4,5},{5,4},{6,7},{7,6},{8,9},{9,8},{10,11... | collective-permute-start | bytes 539144 | tf_op jit(solution)/shard_map/ppermute | solution.py:72
  186.8 4.7 %collective-permute-start.27 = (f32[128,32]{1,0:T(8,128)}, f32[128,32]{1,0:T(8,128)S(1)}, u32[]{:S(2)}, u32[]{:S(2)}) collective-permute-start(f32[128,32]{1,0:T(8,128)} %shard_map.140), channel_id=1, source_target_pairs={{0,4},{1,5},{2,6},{3,7},{4,0},{5,1},{6,2},{7,3},{8,12},{9,13},{10,... | collective-permute-start | bytes 49160 | tf_op jit(solution)/shard_map/ppermute | solution.py:72
  192.4 4.3 %collective-permute-start.28 = (f32[128,32]{1,0:T(8,128)S(1)}, f32[128,32]{1,0:T(8,128)S(1)}, u32[]{:S(2)}, u32[]{:S(2)}) collective-permute-start(f32[128,32]{1,0:T(8,128)S(1)} %add.257), channel_id=1, source_target_pairs={{0,8},{1,9},{2,10},{3,11},{4,12},{5,13},{6,14},{7,15},{8,0},{9,1},... | collective-permute-start | bytes 49160 | tf_op jit(solution)/shard_map/ppermute | solution.py:72
  196.7 5.4 %collective-permute-start.29 = (f32[128,32]{1,0:T(8,128)S(1)}, f32[128,32]{1,0:T(8,128)S(1)}, u32[]{:S(2)}, u32[]{:S(2)}) collective-permute-start(f32[128,32]{1,0:T(8,128)S(1)} %add.258), channel_id=1, source_target_pairs={{0,16},{1,17},{2,18},{3,19},{4,20},{5,21},{6,22},{7,23},{8,24},{9,... | collective-permute-start | bytes 49160 | tf_op jit(solution)/shard_map/ppermute | solution.py:72
  (12 other events, 72.0 us)
